TPU v7x, 32 devices: a whole 2x2x4 slice. The times are simulated.
32 devices in a mesh: seq: 2 (over y), fsdp: 16 (over z, x, core).
Axes of the slice: x: 2, y: 2, z: 4, core: 2. Of those that a mesh axis runs over, the one named last changes fastest.
Arguments:
- block_input: bfloat16 [16, 1024, 768], P('fsdp', 'seq'), may hold values from -6 to 6
- lead_gain: bfloat16 [768], P('fsdp'), may hold values from 0.099609375 to 1.8984375
- joint_weight: bfloat16 [768, 2304], P('fsdp'), may hold values from -0.3125 to 0.3125
- output_weight: bfloat16 [768, 768], P('fsdp'), may hold values from -0.875 to 0.875
- tail_gain: bfloat16 [768], P('fsdp'), may hold values from 0.099609375 to 1.8984375
- up_weight: bfloat16 [768, 3072], P('fsdp'), may hold values from -0.21875 to 0.21875
- down_weight: bfloat16 [3072, 768], P('fsdp'), may hold values from -0.109375 to 0.109375
- cotangent: bfloat16 [16, 1024, 768], P('fsdp', 'seq'), may hold values from -6 to 6
Outputs:
- block_output: bfloat16 [16, 1024, 768], P('fsdp', 'seq')
- input_grad: float32 [16, 1024, 768], P('fsdp', 'seq')
- lead_grad: float32 [768], P('fsdp')
- joint_grad: float32 [768, 2304], P('fsdp')
- output_grad: float32 [768, 768], P('fsdp')
- tail_grad: float32 [768], P('fsdp')
- up_grad: float32 [768, 3072], P('fsdp')
- down_grad: float32 [3072, 768], P('fsdp')
All inputs are finite; a program needn't handle non-finite values.
Results may differ from a plain program's by a relative error of at most 0.014.
The roundings to bfloat16 on the way count: a program that leaves them out, or rounds other values in their place, can miss the bound.
Values may be sent and summed in bfloat16 or wider, within the bound.
No kernel may reach another device: no remote copies, remote signals or barrier semaphores. Data moves between devices by JAX's collectives and lax.ppermute only.
A program may use at most 192 MiB of HBM per device.

v0:
```python
import jax
import jax.numpy as jnp
from jax import lax
from jax.sharding import PartitionSpec as P

D = 768
H = 12
HD = 64


EPS = 1e-05


def norm_rows(values, gain):
    center = values - jnp.mean(values, axis=-1, keepdims=True)
    spread = jnp.mean(center * center, axis=-1, keepdims=True)
    return center * lax.rsqrt(spread + EPS) * gain


def smooth_gate(values):
    return jax.nn.gelu(values, approximate=True)


def outer_sum(left, right):
    return lax.dot_general(
        left, right, (((0,), (0,)), ((), ())), preferred_element_type=jnp.float32
    )


def times_transposed(left, weight):
    return lax.dot_general(
        left, weight, (((1,), (1,)), ((), ())), preferred_element_type=jnp.float32
    )


def body(
    block_input,
    lead_gain,
    joint_weight,
    output_weight,
    tail_gain,
    up_weight,
    down_weight,
    cotangent,
):
    groups = lax.axis_size("seq")
    local = H // groups
    width = local * HD
    tokens = block_input.shape[1]
    length = tokens * groups
    block = min(512, length)
    scale = HD ** (-0.5)
    lead, joint, output, tail, upward, downward = (
        lax.all_gather(lead_gain, "fsdp", axis=0, tiled=True),
        lax.all_gather(joint_weight, "fsdp", axis=0, tiled=True),
        lax.all_gather(output_weight, "fsdp", axis=0, tiled=True),
        lax.all_gather(tail_gain, "fsdp", axis=0, tiled=True),
        lax.all_gather(up_weight, "fsdp", axis=0, tiled=True),
        lax.all_gather(down_weight, "fsdp", axis=0, tiled=True),
    )
    inputs = block_input[0].astype(jnp.float32)
    lead_float = lead.astype(jnp.float32)
    normed_one = norm_rows(inputs, lead_float).astype(jnp.bfloat16)
    projected = jnp.dot(normed_one, joint, preferred_element_type=jnp.float32).astype(jnp.bfloat16)
    regrouped = lax.all_to_all(
        projected.reshape(tokens, 3, groups, width), "seq", split_axis=2, concat_axis=0, tiled=True
    )
    queries = regrouped[:, 0, 0].reshape(length, local, HD)
    keys = regrouped[:, 1, 0].reshape(length, local, HD)
    values = regrouped[:, 2, 0].reshape(length, local, HD)
    spots = jnp.arange(block, dtype=jnp.int32)
    diagonal = spots[None, :] <= spots[:, None]
    pieces = []
    totals = []
    for index in range(length // block):
        start = index * block
        end = start + block
        allowed = jnp.concatenate([jnp.ones((block, start), jnp.bool_), diagonal], axis=1)[None]
        scores = (
            jnp.einsum(
                "qhd,khd->hqk", queries[start:end], keys[:end], preferred_element_type=jnp.float32
            )
            * scale
        )
        safe = jnp.where(allowed, scores, 0.0)
        top = jnp.max(jnp.abs(safe), axis=-1, keepdims=True)
        upper = jnp.where(allowed, jnp.exp(safe - top), 0.0)
        lower = jnp.where(allowed, jnp.exp(-safe - top), 0.0)
        total = top + jnp.log(0.5 * jnp.sum(upper + lower, axis=-1, keepdims=True))
        weights = jnp.where(
            allowed, 0.5 * (jnp.exp(safe - total) - jnp.exp(-safe - total)), 0.0
        ).astype(jnp.bfloat16)
        pieces.append(
            jnp.einsum("hqk,khd->qhd", weights, values[:end], preferred_element_type=jnp.float32)
        )
        totals.append(total)
    heads_out = jnp.concatenate(pieces, axis=0).astype(jnp.bfloat16).reshape(length, width)
    mixed = lax.all_to_all(heads_out, "seq", split_axis=0, concat_axis=1, tiled=True)
    branch = jnp.dot(mixed, output, preferred_element_type=jnp.float32)
    resid = inputs + branch
    tail_float = tail.astype(jnp.float32)
    normed_two = norm_rows(resid, tail_float).astype(jnp.bfloat16)
    pre = jnp.dot(normed_two, upward, preferred_element_type=jnp.float32)
    active = smooth_gate(pre).astype(jnp.bfloat16)
    feed = jnp.dot(active, downward, preferred_element_type=jnp.float32)
    block_output = (resid + feed).astype(jnp.bfloat16)[None]
    lead, joint, output, tail, upward, downward = (
        lax.all_gather(lead_gain, "fsdp", axis=0, tiled=True),
        lax.all_gather(joint_weight, "fsdp", axis=0, tiled=True),
        lax.all_gather(output_weight, "fsdp", axis=0, tiled=True),
        lax.all_gather(tail_gain, "fsdp", axis=0, tiled=True),
        lax.all_gather(up_weight, "fsdp", axis=0, tiled=True),
        lax.all_gather(down_weight, "fsdp", axis=0, tiled=True),
    )
    upstream = cotangent[0]
    down_part = outer_sum(active, upstream)
    dactive = times_transposed(upstream, downward)
    gate_value, gate_back = jax.vjp(smooth_gate, pre)
    dpre = gate_back(dactive)[0].astype(jnp.bfloat16)
    up_part = outer_sum(normed_two, dpre)
    dnormed_two = times_transposed(dpre, upward)
    norm_value, tail_back = jax.vjp(norm_rows, resid, tail_float)
    resid_part, tail_part = tail_back(dnormed_two)
    dresid = upstream.astype(jnp.float32) + resid_part
    dbranch = dresid.astype(jnp.bfloat16)
    output_part = outer_sum(mixed, dbranch)
    dmixed = times_transposed(dbranch, output).astype(jnp.bfloat16)
    dheads = lax.all_to_all(
        dmixed.reshape(tokens, groups, width), "seq", split_axis=1, concat_axis=0, tiled=True
    )
    dheads = dheads.reshape(length, local, HD)
    query_parts = []
    key_grad = jnp.zeros((length, local, HD), jnp.float32)
    value_grad = jnp.zeros((length, local, HD), jnp.float32)
    for index in range(length // block):
        start = index * block
        end = start + block
        allowed = jnp.concatenate([jnp.ones((block, start), jnp.bool_), diagonal], axis=1)[None]
        query_block = queries[start:end]
        upstream_block = dheads[start:end]
        scores = (
            jnp.einsum("qhd,khd->hqk", query_block, keys[:end], preferred_element_type=jnp.float32)
            * scale
        )
        safe = jnp.where(allowed, scores, 0.0)
        total = totals[index]
        grow = jnp.exp(safe - total)
        shrink = jnp.exp(-safe - total)
        signed = jnp.where(allowed, 0.5 * (grow - shrink), 0.0)
        even = jnp.where(allowed, 0.5 * (grow + shrink), 0.0)
        dweights = jnp.einsum(
            "qhd,khd->hqk", upstream_block, values[:end], preferred_element_type=jnp.float32
        )
        inner = jnp.sum(dweights * signed, axis=-1, keepdims=True)
        dscores = (even * dweights - signed * inner).astype(jnp.bfloat16)
        query_parts.append(
            jnp.einsum("hqk,khd->qhd", dscores, keys[:end], preferred_element_type=jnp.float32)
            * scale
        )
        key_grad = key_grad.at[:end].add(
            jnp.einsum("hqk,qhd->khd", dscores, query_block, preferred_element_type=jnp.float32)
            * scale
        )
        value_grad = value_grad.at[:end].add(
            jnp.einsum(
                "hqk,qhd->khd",
                signed.astype(jnp.bfloat16),
                upstream_block,
                preferred_element_type=jnp.float32,
            )
        )
    query_grad = jnp.concatenate(query_parts, axis=0)
    stacked = jnp.stack([query_grad, key_grad, value_grad], axis=1).astype(jnp.bfloat16)
    dprojected = lax.all_to_all(
        stacked.reshape(length, 3, 1, width), "seq", split_axis=0, concat_axis=2, tiled=True
    )
    dprojected = dprojected.reshape(tokens, 3 * D)
    joint_part = outer_sum(normed_one, dprojected)
    dnormed_one = times_transposed(dprojected, joint)
    first_value, lead_back = jax.vjp(norm_rows, inputs, lead_float)
    input_part, lead_part = lead_back(dnormed_one)
    input_grad = (dresid + input_part)[None]
    shards = (
        lax.psum_scatter(lead_part, "fsdp", scatter_dimension=0, tiled=True),
        lax.psum_scatter(joint_part, "fsdp", scatter_dimension=0, tiled=True),
        lax.psum_scatter(output_part, "fsdp", scatter_dimension=0, tiled=True),
        lax.psum_scatter(tail_part, "fsdp", scatter_dimension=0, tiled=True),
        lax.psum_scatter(up_part, "fsdp", scatter_dimension=0, tiled=True),
        lax.psum_scatter(down_part, "fsdp", scatter_dimension=0, tiled=True),
    )
    lead_grad, joint_grad, output_grad, tail_grad, up_grad, down_grad = (
        lax.psum(shards[0].astype(jnp.bfloat16), "seq").astype(jnp.float32),
        lax.psum(shards[1].astype(jnp.bfloat16), "seq").astype(jnp.float32),
        lax.psum(shards[2].astype(jnp.bfloat16), "seq").astype(jnp.float32),
        lax.psum(shards[3].astype(jnp.bfloat16), "seq").astype(jnp.float32),
        lax.psum(shards[4].astype(jnp.bfloat16), "seq").astype(jnp.float32),
        lax.psum(shards[5].astype(jnp.bfloat16), "seq").astype(jnp.float32),
    )
    return (
        block_output,
        input_grad,
        lead_grad,
        joint_grad,
        output_grad,
        tail_grad,
        up_grad,
        down_grad,
    )


def solution(mesh):
    placed = (
        P("fsdp", "seq", None),
        P("fsdp"),
        P("fsdp", None),
        P("fsdp", None),
        P("fsdp"),
        P("fsdp", None),
        P("fsdp", None),
        P("fsdp", "seq", None),
    )
    return jax.shard_map(
        body,
        mesh=mesh,
        in_specs=placed,
        out_specs=(
            P("fsdp", "seq", None),
            P("fsdp", "seq", None),
            P("fsdp"),
            P("fsdp", None),
            P("fsdp", None),
            P("fsdp"),
            P("fsdp", None),
            P("fsdp", None),
        ),
        check_vma=False,
    )
```

profile of v0, /device:TPU:0, one launch (start us, length us, event | category | flops | bytes accessed | tf_op | source)
XLA Modules:
  0.0 759.4 jit_solution(14065129917686234186)
XLA Ops:
  13.1 35.2 %all-reduce.8 = (bf16[768]{0:T(1024)(128)(2,1)S(1)}, bf16[768]{0:T(1024)(128)(2,1)S(1)}) all-reduce(bf16[768]{0:T(1024)(128)(2,1)S(1)} %dynamic-update-slice.10, bf16[768]{0:T(1024)(128)(2,1)S(1)} %dynamic-update-slice.11), channel_id=1, replica_groups=mesh['seq'=2,'fsdp'=16] {'fsdp'}, use_global_device_ids=true, to_apply=%add.3 | all-reduce | flops 1536 | bytes 6144
  51.1 8.8 %all-gather.5.cloned.1.call-done = bf16[768,2304]{1,0:T(8,128)(2,1)} async-done(((bf16[48,2304]{1,0:T(8,128)(2,1)}), bf16[768,2304]{1,0:T(8,128)(2,1)}) %all-gather.5.cloned.1.call-update) | async-done | bytes 3538960 | tf_op jit(solution)/shard_map/all_gather | solution.py:55
  59.9 5.8 convolution_convert_fusion
  65.7 4.6 reshape.331
  72.1 3.8 all-to-all-start
  77.8 26.4 %all-to-all-done = bf16[512,3,2,384]{3,0,1,2:T(8,128)(2,1)S(1)} async-done(((bf16[512,3,2,384]{3,0,1,2:T(8,128)(2,1)}), bf16[512,3,2,384]{3,0,1,2:T(8,128)(2,1)S(1)}, u32[]{:S(2)}, u32[]{:S(2)}) %all-to-all-start) | async-done | bytes 2359328 | tf_op jit(solution)/shard_map/all_to_all | solution.py:65
  110.7 3.0 add_reduce_fusion.1
  113.7 2.7 fusion.14
  119.8 4.3 abs_reduce_fusion
  124.1 6.7 add_reduce_fusion
  130.9 6.4 fusion.7
  137.3 2.6 copy-done.1
  140.0 2.8 convolution_convert_fusion.2
  146.8 4.3 all-to-all-start.1
  151.1 10.8 %all-to-all-done.1 = bf16[2,512,384]{2,1,0:T(8,128)(2,1)} async-done(((bf16[2,512,384]{2,1,0:T(8,128)(2,1)}), bf16[2,512,384]{2,1,0:T(8,128)(2,1)}, u32[]{:S(2)}, u32[]{:S(2)}) %all-to-all-start.1) | async-done | bytes 786464 | tf_op jit(solution)/shard_map/all_to_all | solution.py:98
  161.8 2.3 copy.70
  164.2 2.6 fusion.59
  168.3 8.2 %fusion.53 = f32[512,3072]{1,0:T(8,128)} fusion(bf16[768,3072]{1,0:T(8,128)(2,1)} %all-gather.9.cloned.1.call-done, f32[512,768]{1,0:T(8,128)} %copy-done.5, f32[768]{0:T(1024)S(1)} %convert_element_type.117, f32[512]{0:T(512)S(1)} %fusion.50, f32[512]{0:T(512)S(1)} %broadcast_multiply_fusion), kind=kOutput, calls=%fused_computation.107 | convolution fusion | flops 2417491968 | bytes 12590080 | tf_op jit(solution)/shard_map/dot_general | solution.py:103
  176.5 31.9 %all-gather.11.cloned.1.call-done = bf16[3072,768]{1,0:T(8,128)(2,1)} async-done(((bf16[192,768]{1,0:T(8,128)(2,1)}), bf16[3072,768]{1,0:T(8,128)(2,1)}) %all-gather.11.cloned.1.call-update) | async-done | bytes 4718608 | tf_op jit(solution)/shard_map/all_gather | solution.py:59
  208.5 8.7 %fusion.6 = bf16[512,3072]{1,0:T(8,128)(2,1)S(1)} fusion(f32[512,3072]{1,0:T(8,128)} %fusion.53, bf16[3072,768]{1,0:T(8,128)(2,1)} %all-gather.11.cloned.1.call-done, bf16[1,512,768]{2,1,0:T(8,128)(2,1)} %param.27), kind=kOutput, calls=%fused_computation.16 | convolution fusion | flops 2447376384 | bytes 14942208 | tf_op jit(solution)/shard_map/dot_general | solution.py:31
  217.3 3.4 multiply_reduce_fusion.2
  225.5 4.3 all-to-all-start.2
  230.0 3.6 fusion.60
  233.6 7.7 %all-to-all-done.2 = bf16[512,2,384]{2,0,1:T(8,128)(2,1)} async-done(((bf16[512,2,384]{2,0,1:T(8,128)(2,1)}), bf16[512,2,384]{2,0,1:T(8,128)(2,1)}, u32[]{:S(2)}, u32[]{:S(2)}) %all-to-all-start.2) | async-done | bytes 786464 | tf_op jit(solution)/shard_map/all_to_all | solution.py:128
  245.4 3.0 convolution_bitcast_fusion
  248.4 9.3 %multiply_reduce_fusion.1 = (f32[6,512]{1,0:T(8,128)S(1)}, f32[6,512,512]{1,2,0:T(8,128)}) fusion(f32[6,512]{1,0:T(8,128)S(1)} %log_add_fusion.1, f32[6,512,512]{1,2,0:T(8,128)} %copy-done.2, pred[512,512]{0,1:T(8,128)(4,1)S(1)} %iota_compare_fusion, bf16[512,6,64]{0,2,1:T(8,128)(2,1)} %bitcast.171, bf16[512,6,64]{0,2,1:T(8,128)(2,1)} %bitcast.174), kind=kOutput, calls=%fused_computation.18 | convolution fusion | flops 217052160 | bytes 13656064 | tf_op jit(solution)/shard_map/qhd,khd->hqk/dot_general | solution.py:151
  258.9 13.4 %multiply_reduce_fusion = (f32[6,512]{1,0:T(8,128)S(1)}, f32[6,512,1024]{2,1,0:T(8,128)}) fusion(f32[6,512]{1,0:T(8,128)S(1)} %log_add_fusion, f32[6,512,1024]{2,1,0:T(8,128)} %copy-done, pred[512,1024]{1,0:T(8,128)(4,1)S(1)} %copy-done.10, bf16[512,6,64]{0,2,1:T(8,128)(2,1)S(1)} %bitcast.165, bf16[1024,6,64]{0,2,1:T(8,128)(2,1)} %bitcast.154), kind=kOutput, calls=%fused_computation.1 | convolution fusion | flops 434107392 | bytes 26894336 | tf_op jit(solution)/shard_map/qhd,khd->hqk/dot_general | solution.py:151
  274.5 6.5 subtract_convert_fusion.1
  281.0 12.0 %subtract_convert_fusion = bf16[6,512,1024]{2,1,0:T(8,128)(2,1)} fusion(f32[6,512,1024]{2,1,0:T(8,128)} %get-tuple-element.108, f32[6,512,1024]{2,1,0:T(8,128)S(1)} %bitcast.144, f32[6,512]{1,0:T(8,128)S(1)} %get-tuple-element.107, f32[6,512]{1,0:T(8,128)S(1)} %log_add_fusion, pred[512,1024]{1,0:T(8,128)(4,1)S(1)} %copy-done.11), kind=kLoop, calls=%fused_computation | loop fusion | flops 47185920 | bytes 32006144 | tf_op jit(solution)/shard_map/convert_element_type | solution.py:155
  295.0 4.8 copy.79
  299.8 5.0 fusion.25
  304.9 5.1 copy.78
  311.6 5.2 fusion.31
  317.8 4.8 copy.77
  322.6 6.8 pad_maximum_fusion
  329.4 38.3 %all_to_all.64 = bf16[1024,3,1,384]{3,1,2,0:T(4,128)(2,1)S(1)} all-to-all(bf16[1024,3,1,384]{3,1,2,0:T(4,128)(2,1)S(1)} %pad_maximum_fusion), channel_id=1, replica_groups=mesh['seq'=2,'fsdp'=16] {'seq'}, dimensions={0} | all-to-all | bytes 4718592 | tf_op jit(solution)/shard_map/all_to_all | solution.py:174
  369.4 4.3 copy.81
  373.7 7.0 fusion.34
  380.8 10.1 %fusion.37 = f32[3072,768]{1,0:T(8,128)} fusion(bf16[1,512,768]{2,1,0:T(8,128)(2,1)S(1)} %copy-done.17, f32[512,3072]{1,0:T(8,128)} %fusion.53), kind=kOutput, calls=%fused_computation.81 | convolution fusion | flops 2430074880 | bytes 16515072 | tf_op jit(solution)/shard_map/dot_general | solution.py:25
  392.4 7.5 fusion.52
  400.9 8.9 %fusion.26 = bf16[1,512,768]{2,1,0:T(8,128)(2,1)} fusion(f32[512,768]{1,0:T(8,128)S(1)} %copy-done.7, bf16[3072,768]{1,0:T(8,128)(2,1)} %all-gather.11.cloned.1.call-done, f32[512,3072]{1,0:T(8,128)} %fusion.53), kind=kOutput, calls=%fused_computation.62 | convolution fusion | flops 2430861312 | bytes 13369344 | tf_op jit(solution)/shard_map/dot_general | solution.py:105
  409.8 3.3 fusion.20
  414.8 53.9 %reduce-scatter.5.cloned.1.call-done = f32[48,2304]{1,0:T(8,128)} async-done(((f32[768,2304]{1,0:T(8,128)}), f32[48,2304]{1,0:T(8,128)}) %reduce-scatter.5.cloned.1.call-update) | async-done | bytes 442384 | tf_op jit(solution)/shard_map/reduce_scatter | solution.py:185
  470.4 113.3 %reduce-scatter.11.cloned.1.call-done = f32[192,768]{1,0:T(8,128)} async-done(((f32[3072,768]{1,0:T(8,128)}), f32[192,768]{1,0:T(8,128)}) %reduce-scatter.11.cloned.1.call-update) | async-done | bytes 589840 | tf_op jit(solution)/shard_map/reduce_scatter | solution.py:189
  585.5 114.0 %reduce-scatter.9.cloned.1.call-done = f32[48,3072]{1,0:T(8,128)} async-done(((f32[768,3072]{1,0:T(8,128)}), f32[48,3072]{1,0:T(8,128)}) %reduce-scatter.9.cloned.1.call-update) | async-done | bytes 589840 | tf_op jit(solution)/shard_map/reduce_scatter | solution.py:188
  703.5 32.7 %all-reduce.7 = (bf16[768]{0:T(1024)(128)(2,1)S(1)}, bf16[768]{0:T(1024)(128)(2,1)S(1)}) all-reduce(f32[768]{0:T(1024)S(1)} %get-tuple-element.74, f32[768]{0:T(1024)S(1)} %copy-done.35), channel_id=2, replica_groups=mesh['seq'=2,'fsdp'=16] {'fsdp'}, use_global_device_ids=true, to_apply=%region_15.16.clone | all-reduce | flops 1536 | bytes 9216
  736.4 4.9 all-reduce.9
  742.3 3.2 add_bitcast_fusion
  (174 shorter events, 65.0 us)
Async XLA Ops:
  7.2 52.8 %all-gather.5.cloned.1.call-start = ((), (), s32[]{:S(2)}) async-start(), calls=%async_computation.8 | async-start | bytes 3760128 | tf_op jit(solution)/shard_map/all_gather | solution.py:55
  7.9 156.3 %all-gather.7.cloned.1.call-start = ((), (), s32[]{:S(2)}) async-start(), calls=%async_computation.9 | async-start | bytes 1253376 | tf_op jit(solution)/shard_map/all_gather | solution.py:56
  8.6 159.6 %all-gather.9.cloned.1.call-start = ((), (), s32[]{:S(2)}) async-start(), calls=%async_computation.10 | async-start | bytes 5013504 | tf_op jit(solution)/shard_map/all_gather | solution.py:58
  49.6 10.4 %copy-start.27 = (f32[512]{0:T(512)}, f32[512]{0:T(512)S(1)}, u32[]{:S(2)}) copy-start(f32[512]{0:T(512)S(1)} %broadcast_multiply_fusion.1) | copy-start | bytes 6148
  51.1 8.9 %copy-start.33 = (f32[512]{0:T(512)}, f32[512]{0:T(512)S(1)}, u32[]{:S(2)}) copy-start(f32[512]{0:T(512)S(1)} %fusion.19) | copy-start | bytes 6148
  51.1 8.9 %copy-start.29 = (f32[512]{0:T(512)}, f32[512]{0:T(512)S(1)}, u32[]{:S(2)}) copy-start(f32[512]{0:T(512)S(1)} %fusion.49) | copy-start | bytes 6148
  72.1 32.1 %all-to-all-start = ((bf16[512,3,2,384]{3,0,1,2:T(8,128)(2,1)}), bf16[512,3,2,384]{3,0,1,2:T(8,128)(2,1)S(1)}, u32[]{:S(2)}, u32[]{:S(2)}) async-start(bf16[512,3,2,384]{3,0,1,2:T(8,128)(2,1)} %copy.58), calls=%async_computation | async-start | bytes 4718592 | tf_op jit(solution)/shard_map/all_to_all | solution.py:65
  75.9 132.6 %all-gather.11.cloned.1.call-start = ((), (), s32[]{:S(2)}) async-start(), calls=%async_computation.11 | async-start | bytes 5013504 | tf_op jit(solution)/shard_map/all_gather | solution.py:59
  106.2 7.4 copy-start.25
  107.4 6.3 copy-start.23
  110.7 5.8 copy-start.2
  119.8 4.3 copy-start.9
  124.1 6.8 copy-start
  130.9 9.1 %copy-start.15 = (bf16[1024,1,1,384]{0,3,2,1:T(8,128)(2,1)S(1)}, bf16[1024,1,1,384]{0,3,2,1:T(8,128)(2,1)}, u32[]{:S(2)}) copy-start(bf16[1024,1,1,384]{0,3,2,1:T(8,128)(2,1)} %copy.64) | copy-start | bytes 2359300
  146.8 15.1 %all-to-all-start.1 = ((bf16[2,512,384]{2,1,0:T(8,128)(2,1)}), bf16[2,512,384]{2,1,0:T(8,128)(2,1)}, u32[]{:S(2)}, u32[]{:S(2)}) async-start(bf16[2,512,384]{2,1,0:T(8,128)(2,1)} %bitcast.157), calls=%async_computation.1 | async-start | bytes 1572864 | tf_op jit(solution)/shard_map/all_to_all | solution.py:98
  208.5 8.8 %copy-start.6 = (f32[512,768]{1,0:T(8,128)S(1)}, f32[512,768]{1,0:T(8,128)}, u32[]{:S(2)}) copy-start(f32[512,768]{1,0:T(8,128)} %copy-done.5) | copy-start | bytes 4718596
  208.5 8.8 %copy-start.36 = (bf16[768,3072]{1,0:T(8,128)(2,1)S(1)}, bf16[768,3072]{1,0:T(8,128)(2,1)}, u32[]{:S(2)}) copy-start(bf16[768,3072]{1,0:T(8,128)(2,1)} %all-gather.9.cloned.1.call-done) | copy-start | bytes 14155780
  217.2 3.4 copy-start.19
  217.3 5.3 copy-start.16
  221.4 12.2 %copy-start.31 = (f32[512]{0:T(512)}, f32[512]{0:T(512)S(1)}, u32[]{:S(2)}) copy-start(f32[512]{0:T(512)S(1)} %negate_multiply_fusion.1) | copy-start | bytes 6148
  225.5 15.9 %all-to-all-start.2 = ((bf16[512,2,384]{2,0,1:T(8,128)(2,1)}), bf16[512,2,384]{2,0,1:T(8,128)(2,1)}, u32[]{:S(2)}, u32[]{:S(2)}) async-start(bf16[512,2,384]{2,0,1:T(8,128)(2,1)} %bitcast.156), calls=%async_computation.2 | async-start | bytes 1572864 | tf_op jit(solution)/shard_map/all_to_all | solution.py:128
  229.8 183.4 %reduce-scatter.7.cloned.1.call-start = ((), (), s32[]{:S(2)}) async-start(), calls=%async_computation.13 | async-start | bytes 2506752 | tf_op jit(solution)/shard_map/reduce_scatter | solution.py:186
  233.6 235.1 %reduce-scatter.5.cloned.1.call-start = ((), (), s32[]{:S(2)}) async-start(), calls=%async_computation.12 | async-start | bytes 7520256 | tf_op jit(solution)/shard_map/reduce_scatter | solution.py:185
  248.4 10.5 %copy-start.10 = (pred[512,1024]{1,0:T(8,128)(4,1)S(1)}, pred[512,1024]{1,0:T(8,128)(4,1)}, u32[]{:S(2)}) copy-start(pred[512,1024]{1,0:T(8,128)(4,1)} %concatenate.34.clone) | copy-start | bytes 1572868
  248.4 23.9 %slice-start.3 = ((s8[6291456]{0:T(1024)(128)(4,1)}), s8[2097152]{0:T(1024)(128)(4,1)S(1)}, s32[]{:S(2)}) async-start(s8[6291456]{0:T(1024)(128)(4,1)} %bitcast.145), calls=%async_computation.20 | async-start | bytes 4194304
  258.9 13.5 %slice-start.4 = ((s8[6291456]{0:T(1024)(128)(4,1)}), s8[4194304]{0:T(1024)(128)(4,1)S(1)}, s32[]{:S(2)}) async-start(s8[6291456]{0:T(1024)(128)(4,1)} %bitcast.145), calls=%async_computation.21 | async-start | bytes 8388608
  258.9 13.5 %copy-start.20 = (f32[512,6,64]{0,2,1:T(8,128)S(1)}, f32[512,6,64]{0,2,1:T(8,128)}, u32[]{:S(2)}) copy-start(f32[512,6,64]{0,2,1:T(8,128)} %convolution_bitcast_fusion) | copy-start | bytes 2359300
  258.9 15.6 %copy-start.12 = (f32[6,512,512]{1,2,0:T(8,128)S(1)}, f32[6,512,512]{1,2,0:T(8,128)}, u32[]{:S(2)}) copy-start(f32[6,512,512]{1,2,0:T(8,128)} %get-tuple-element.106) | copy-start | bytes 18874372
  272.3 8.7 %slice-start = ((s8[12582912]{0:T(1024)(128)(4,1)}), s8[4194304]{0:T(1024)(128)(4,1)S(1)}, s32[]{:S(2)}) async-start(s8[12582912]{0:T(1024)(128)(4,1)} %bitcast.143), calls=%async_computation.17 | async-start | bytes 8388608
  272.4 8.7 %slice-start.1 = ((s8[12582912]{0:T(1024)(128)(4,1)}), s8[4194304]{0:T(1024)(128)(4,1)S(1)}, s32[]{:S(2)}) async-start(s8[12582912]{0:T(1024)(128)(4,1)} %bitcast.143), calls=%async_computation.18 | async-start | bytes 8388608
  274.5 6.6 slice-start.2
  274.5 6.6 copy-start.11
  281.0 12.0 %copy-start.24 = (bf16[512,1,1,384]{0,3,2,1:T(8,128)(2,1)S(1)}, bf16[512,1,1,384]{0,3,2,1:T(8,128)(2,1)}, u32[]{:S(2)}) copy-start(bf16[512,1,1,384]{0,3,2,1:T(8,128)(2,1)} %copy-done.23) | copy-start | bytes 1179652
  293.0 6.8 copy-start.22
  311.6 11.0 %copy-start.13 = (bf16[1024,1,1,384]{3,1,2,0:T(2,128)(2,1)S(1)}, bf16[1024,1,1,384]{3,1,2,0:T(2,128)(2,1)}, u32[]{:S(2)}) copy-start(bf16[1024,1,1,384]{3,1,2,0:T(2,128)(2,1)} %copy.79) | copy-start | bytes 2359300
  311.6 11.0 %copy-start.14 = (bf16[1024,1,1,384]{3,1,2,0:T(2,128)(2,1)S(1)}, bf16[1024,1,1,384]{3,1,2,0:T(2,128)(2,1)}, u32[]{:S(2)}) copy-start(bf16[1024,1,1,384]{3,1,2,0:T(2,128)(2,1)} %copy.78) | copy-start | bytes 2359300
  367.7 6.1 copy-start.8
  367.7 6.1 copy-start.28
  367.7 6.1 copy-start.30
  373.7 7.1 copy-start.17
  380.8 202.9 %reduce-scatter.11.cloned.1.call-start = ((), (), s32[]{:S(2)}) async-start(), calls=%async_computation.15 | async-start | bytes 10027008 | tf_op jit(solution)/shard_map/reduce_scatter | solution.py:189
  390.9 308.6 %reduce-scatter.9.cloned.1.call-start = ((), (), s32[]{:S(2)}) async-start(), calls=%async_computation.14 | async-start | bytes 10027008 | tf_op jit(solution)/shard_map/reduce_scatter | solution.py:188
  399.9 345.7 %all-reduce.13.cloned.1.call-start = ((), (), s32[]{:S(2)}) async-start(), calls=%async_computation.16 | async-start | bytes 1769472 | tf_op jit(solution)/shard_map/psum | solution.py:193
  400.8 8.9 %copy-start.21 = (bf16[512,3,2,1,384]{0,4,2,1,3:T(8,128)(2,1)S(1)}, bf16[512,3,2,1,384]{0,4,2,1,3:T(8,128)(2,1)}, u32[]{:S(2)}) copy-start(bf16[512,3,2,1,384]{0,4,2,1,3:T(8,128)(2,1)} %copy.81) | copy-start | bytes 7077892
  400.8 8.9 %copy-start.37 = (bf16[768,2304]{1,0:T(8,128)(2,1)S(1)}, bf16[768,2304]{1,0:T(8,128)(2,1)}, u32[]{:S(2)}) copy-start(bf16[768,2304]{1,0:T(8,128)(2,1)} %all-gather.5.cloned.1.call-done) | copy-start | bytes 10616836
  409.8 293.7 %copy-start.35 = (f32[768]{0:T(1024)S(1)}, f32[768]{0:T(1024)}, u32[]{:S(2)}) copy-start(f32[768]{0:T(1024)} %get-tuple-element.72) | copy-start | bytes 9220
  409.8 332.5 %copy-start.32 = (f32[512]{0:T(512)S(1)}, f32[512]{0:T(512)}, u32[]{:S(2)}) copy-start(f32[512]{0:T(512)} %copy-done.31) | copy-start | bytes 6148
  413.1 329.2 %copy-start.4 = (f32[512,768]{1,0:T(8,128)S(1)}, f32[512,768]{1,0:T(8,128)}, u32[]{:S(2)}) copy-start(f32[512,768]{1,0:T(8,128)} %copy-done.3) | copy-start | bytes 4718596
  (8 other events, 16.5 us)
Sparse Core Ops, SparseCore 0:
  10.3 49.6 all-gather.4
  62.2 37.5 all-gather.6
  102.1 52.2 all-gather.8
  156.5 51.9 all-gather.10
  234.1 62.0 reduce-scatter.6
  380.9 87.7 reduce-scatter.4
  472.8 110.8 reduce-scatter.10
  588.3 111.0 reduce-scatter.8
  702.6 36.8 all-reduce.12
where the time goes:
time: 767 us; the launch traced here: 759 us
  waiting for transfers between devices  369 us (48%)
  matrix products  121 us (16%)
  blocking collectives  111 us (14%)
  other arithmetic  71.7 us (9%)
  local copies, waits for them, and re-layouts  56.6 us (7%)
  between operations  16.3 us (2%)
  starting transfers between devices  13.2 us (2%)
    reduce_scatter x1, waiting for transfers between devices, body(): lax.psum_scatter(up_part, 'fsdp', scatter_dimension=0, tiled=True)  114 us
    reduce_scatter x1, waiting for transfers between devices, body(): lax.psum_scatter(down_part, 'fsdp', scatter_dimension=0, tiled=True)  113 us
    unnamed x2, blocking collectives  67.9 us
    reduce_scatter x1, waiting for transfers between devices, body(): lax.psum_scatter(joint_part, 'fsdp', scatter_dimension=0, tiled=True)  53.9 us
    all_to_all x1, blocking collectives, body(): lax.all_to_all(stacked.reshape(length, 3, 1, width), 'seq', split_axis=0,...  38.3 us
    all_gather x1, waiting for transfers between devices, body(): lax.all_gather(down_weight, 'fsdp', axis=0, tiled=True)  31.9 us
    dot_general x4, matrix products, outer_sum(): lax.dot_general(left, right, (((0,), (0,)), ((), ())), preferred_element_...  28.1 us
    all_to_all x1, waiting for transfers between devices, body(): lax.all_to_all(projected.reshape(tokens, 3, groups, width), 'seq', split_...  26.4 us
  transfers between devices with their start and end apart: 12, of which 8 were waited for; matrix products, arithmetic and copies ran while one was open for 29% of the time, Pallas kernels for 0%

commit v1 on v0

v1 whole, which is shorter than its diff:
```python
import jax
import jax.numpy as jnp
from jax import lax
from jax.experimental import pallas as pl
from jax.experimental.pallas import tpu as pltpu
from jax.sharding import PartitionSpec as P

HD = 64
EPS = 1e-05
PAIR = 2 * HD
BAND = 256
LOG2E = 1.4426950408889634
LIMIT = 56 << 20
F32 = jnp.float32
BF16 = jnp.bfloat16

VMEM = pl.BlockSpec(memory_space=pltpu.VMEM)
SMEM = pl.BlockSpec(memory_space=pltpu.SMEM)


def dot(left, right):
    return jnp.dot(left, right, preferred_element_type=F32)


def dot_t(left, right):
    return lax.dot_general(left, right, (((1,), (1,)), ((), ())), preferred_element_type=F32)


def shaped(*dims, dtype=BF16):
    return jax.ShapeDtypeStruct(dims, dtype)


def cost(microseconds):
    return pl.CostEstimate(flops=int(microseconds * 1e9), transcendentals=0, bytes_accessed=int(microseconds * 3e6))


def call(kernel, name, outs, n_in, scratch=(), took=4):
    return pl.pallas_call(
        kernel,
        name=name,
        out_shape=outs,
        in_specs=[SMEM] + [VMEM] * n_in,
        out_specs=[VMEM] * len(outs),
        scratch_shapes=list(scratch),
        compiler_params=pltpu.CompilerParams(vmem_limit_bytes=LIMIT),
        cost_estimate=cost(took),
    )


def standardize(values):
    center = values - jnp.mean(values, axis=-1, keepdims=True)
    spread = jnp.mean(center * center, axis=-1, keepdims=True)
    rstd = lax.rsqrt(spread + EPS)
    return center * rstd, rstd


def norm_back(z, rstd, g):
    return (g - jnp.mean(g, axis=-1, keepdims=True) - z * jnp.mean(g * z, axis=-1, keepdims=True)) * rstd


def half_at(index, size):
    return pl.ds(pl.multiple_of(index * size, size), size)


def rows_in_order(meta, source, target, count, size):
    for spot in range(count):
        target[spot * size : (spot + 1) * size, :] = source[pl.ds(pl.multiple_of(meta[1 + spot] * size, size), size), :]


def first_norm(meta, own, other, gains, zb, zt, turned):
    half = own.shape[0]
    for source, place in ((own, meta[0]), (other, 1 - meta[0])):
        z = (standardize(source[...].astype(F32))[0] * gains[0:1, :].astype(F32)).astype(BF16)
        zb[half_at(place, half), :] = z
        turned[:, half_at(place, half)] = z.T
    rows_in_order(meta, turned, zt, 16, turned.shape[0] // 16)


def attend(meta, zb, near, far, qkv, o_own, o_other, lse, weight, km, vt, s_sc, p_sc, ot, o_all):
    length = zb.shape[0]
    half = length // 2
    size = weight.shape[0] // 16
    for spot in range(16):
        source = (near, far)[spot // 8]
        target = pl.ds(pl.multiple_of(meta[26 + spot] * size, size), size)
        weight[target, :] = source[spot % 8 * size : (spot % 8 + 1) * size, :]
    qkv[...] = dot(zb[...], weight[...]).astype(BF16)
    lane = lax.broadcasted_iota(jnp.int32, (1, PAIR), 1)
    keys = qkv[:, PAIR : 2 * PAIR]
    zero = jnp.zeros_like(keys)
    km[0] = jnp.where(lane < HD, keys, zero)
    km[1] = jnp.where(lane < HD, zero, keys)
    vt[...] = qkv[:, 2 * PAIR :].T
    lse[...] = jnp.zeros_like(lse)
    allowed = lax.broadcasted_iota(jnp.int32, (BAND, BAND), 0) <= lax.broadcasted_iota(jnp.int32, (BAND, BAND), 1)
    for q_band in range(length // BAND):
        spots = slice(q_band * BAND, (q_band + 1) * BAND)
        queries = qkv[spots, :PAIR]
        for head in range(2):
            top = None
            for k_band in range(q_band + 1):
                rows = slice(k_band * BAND, (k_band + 1) * BAND)
                s = dot_t(km[head, rows, :], queries) * (HD ** -0.5 * LOG2E)
                if k_band == q_band:
                    s = jnp.where(allowed, s, 0.0)
                s_sc[rows, :] = s
                peak = jnp.max(jnp.abs(s), axis=0, keepdims=True)
                top = peak if top is None else jnp.maximum(top, peak)
            total = None
            for k_band in range(q_band + 1):
                rows = slice(k_band * BAND, (k_band + 1) * BAND)
                s = s_sc[rows, :]
                grow = jnp.exp2(s - top)
                shrink = jnp.exp2(-s - top)
                p_sc[rows, :] = (grow - shrink).astype(BF16)
                both = grow + shrink
                if k_band == q_band:
                    both = jnp.where(allowed, both, 0.0)
                part = jnp.sum(both, axis=0, keepdims=True)
                total = part if total is None else total + part
            end = (q_band + 1) * BAND
            mine = slice(head * HD, (head + 1) * HD)
            ot[mine, :] = dot(vt[mine, :end], p_sc[:end, :]) / total
            lse[head : head + 1, spots] = top + jnp.log2(0.5 * total)
        o_all[spots, :] = ot[...].T.astype(BF16)
    o_own[...] = o_all[half_at(meta[0], half), :]
    o_other[...] = o_all[half_at(1 - meta[0], half), :]


def attend_back(
    meta, qkv, o_own, o_other, d_own, d_other, lse, zt, g_own, g_other, keep, send, km, vm, kt, do, inner, dk, dv, dqt, dqkv
):
    length = qkv.shape[0]
    half = length // 2
    lane = lax.broadcasted_iota(jnp.int32, (1, PAIR), 1)
    low = lane < HD
    keys = qkv[:, PAIR : 2 * PAIR]
    values = qkv[:, 2 * PAIR :]
    zero = jnp.zeros_like(keys)
    km[0] = jnp.where(low, keys, zero)
    km[1] = jnp.where(low, zero, keys)
    vm[0] = jnp.where(low, values, zero)
    vm[1] = jnp.where(low, zero, values)
    kt[...] = keys.T
    pick = (
        lax.broadcasted_iota(jnp.int32, (8, PAIR), 1) // HD == lax.broadcasted_iota(jnp.int32, (8, PAIR), 0)
    ).astype(F32)
    for o_part, d_part, place in ((o_own, d_own, meta[0]), (o_other, d_other, 1 - meta[0])):
        do[half_at(place, half), :] = d_part[...]
        product = o_part[...].astype(F32) * d_part[...].astype(F32)
        inner[:, half_at(place, half)] = lax.dot_general(
            pick, product, (((1,), (1,)), ((), ())), preferred_element_type=F32, precision=lax.Precision.HIGHEST
        )
    allowed = lax.broadcasted_iota(jnp.int32, (BAND, BAND), 0) <= lax.broadcasted_iota(jnp.int32, (BAND, BAND), 1)
    small = jnp.zeros((BAND, PAIR), BF16)
    for q_band in range(length // BAND):
        spots = slice(q_band * BAND, (q_band + 1) * BAND)
        queries = qkv[spots, :PAIR]
        upstream = do[spots, :]
        for head in range(2):
            mine = slice(head * HD, (head + 1) * HD)
            q_mine = jnp.where(low, queries, small) if head == 0 else jnp.where(low, small, queries)
            d_mine = jnp.where(low, upstream, small) if head == 0 else jnp.where(low, small, upstream)
            base = lse[head : head + 1, spots] + 1.0
            mean = inner[head : head + 1, spots]
            for k_band in range(q_band + 1):
                rows = slice(k_band * BAND, (k_band + 1) * BAND)
                s = dot_t(km[head, rows, :], queries) * (HD ** -0.5 * LOG2E)
                dw = dot_t(vm[head, rows, :], upstream)
                if k_band == q_band:
                    s = jnp.where(allowed, s, 0.0)
                    dw = jnp.where(allowed, dw, 0.0)
                grow = jnp.exp2(s - base)
                shrink = jnp.exp2(-s - base)
                p = grow - shrink
                ds = ((grow + shrink) * dw - p * mean).astype(BF16)
                dv_part = dot(p.astype(BF16), d_mine)
                dk_part = dot(ds, q_mine)
                dq_part = dot(kt[mine, rows], ds)
                if q_band == k_band and head == 0:
                    dv[rows, :] = dv_part
                    dk[rows, :] = dk_part
                else:
                    dv[rows, :] += dv_part
                    dk[rows, :] += dk_part
                if k_band == 0:
                    dqt[mine, :] = dq_part
                else:
                    dqt[mine, :] += dq_part
        dqkv[spots, :PAIR] = (dqt[...].T * HD ** -0.5).astype(BF16)
    dqkv[:, PAIR : 2 * PAIR] = (dk[...] * HD ** -0.5).astype(BF16)
    dqkv[:, 2 * PAIR :] = dv[...].astype(BF16)
    g_own[...] = dqkv[half_at(meta[0], half), :]
    g_other[...] = dqkv[half_at(1 - meta[0], half), :]
    middle = keep.shape[0]
    send[...] = dot(zt[middle:, :], dqkv[...]).astype(BF16)
    keep[...] = dot(zt[:middle, :], dqkv[...]).astype(BF16)


def project_out(meta, own, o0, o1, o2, r0, r1, r2, gains, weight, resid, zb, zt, mt, mixed, turned):
    for spot, (mine, other) in enumerate(((o0, r0), (o1, r1), (o2, r2))):
        mixed[:, pl.ds(pl.multiple_of(meta[0] * 3 * PAIR + spot * PAIR, PAIR), PAIR)] = mine[...]
        mixed[:, pl.ds(pl.multiple_of((1 - meta[0]) * 3 * PAIR + spot * PAIR, PAIR), PAIR)] = other[...]
    summed = own[...].astype(F32) + dot(mixed[...], weight[...])
    resid[...] = summed
    z = (standardize(summed)[0] * gains[1:2, :].astype(F32)).astype(BF16)
    zb[...] = z
    size = turned.shape[0] // 16
    turned[...] = z.T
    rows_in_order(meta, turned, zt, 16, size)
    turned[...] = mixed[...].T
    rows_in_order(meta, turned, mt, 16, size)


def feed(
    meta, zb, zt, up, down, upstream, resid, out, g_out, up_keep, up_send, down_keep, down_send, feed_acc, g_acc, turned, picked
):
    step = pl.program_id(0)
    v = dot(zb[...], up[...])
    root = 0.7978845608028654
    square = v * v
    t = jnp.tanh(root * v * (1.0 + 0.044715 * square))
    cdf = 0.5 * (1.0 + t)
    active = (v * cdf).astype(BF16)
    slope = cdf + v * (0.5 * root) * (1.0 - t * t) * (1.0 + 0.134145 * square)
    dpre = (dot_t(upstream[...], down[...]) * slope).astype(BF16)
    feed_part = dot(active, down[...])
    g_part = dot_t(dpre, up[...])
    middle = up_keep.shape[0]
    up_keep[...] = dot(zt[:middle, :], dpre).astype(BF16)
    up_send[...] = dot(zt[middle:, :], dpre).astype(BF16)
    turned[...] = active.T
    size = turned.shape[0] // 8
    for spot in range(8):
        block = meta[17 + spot]
        picked[spot * size : (spot + 1) * size, :] = turned[pl.ds(pl.multiple_of(block * size, size), size), :]
    middle = turned.shape[0] // 2
    down_keep[0] = dot(picked[:middle, :], upstream[...]).astype(BF16)
    down_send[0] = dot(picked[middle:, :], upstream[...]).astype(BF16)

    @pl.when(step == 0)
    def _():
        feed_acc[...] = feed_part
        g_acc[...] = g_part

    @pl.when(step > 0)
    def _():
        feed_acc[...] += feed_part
        g_acc[...] += g_part

    @pl.when(step == pl.num_programs(0) - 1)
    def _():
        out[...] = (resid[...] + feed_acc[...]).astype(BF16)
        g_out[...] = g_acc[...]


def branch_back(meta, g, resid, upstream, gains, weight, dresid, db, s0, s1, s2, m0, m1, m2):
    z, rstd = standardize(resid[...])
    grad = upstream[...].astype(F32) + norm_back(z, rstd, g[...] * gains[1:2, :].astype(F32))
    dresid[...] = grad
    low = grad.astype(BF16)
    db[...] = low
    for side, targets in ((1 - meta[0], (s0, s1, s2)), (meta[0], (m0, m1, m2))):
        part = dot_t(low, weight[half_at(side, 3 * PAIR), :]).astype(BF16)
        for spot, target in enumerate(targets):
            target[...] = part[:, spot * PAIR : (spot + 1) * PAIR]


def output_back(meta, mt, db, keep, send):
    middle = keep.shape[0]
    send[...] = dot(mt[middle:, :], db[...]).astype(BF16)
    keep[...] = dot(mt[:middle, :], db[...]).astype(BF16)


def token_back(meta, g0, g1, g2, w0, w1, w2, out):
    out[...] = (dot_t(g0[...], w0[...]) + dot_t(g1[...], w1[...]) + dot_t(g2[...], w2[...])).astype(out.dtype)


def input_back(meta, own, mine, other, dresid, gains, out):
    z, rstd = standardize(own[...].astype(F32))
    g = (mine[...] + other[...].astype(F32)) * gains[0:1, :].astype(F32)
    out[...] = dresid[...] + norm_back(z, rstd, g)


SWAP = [(0, 1), (1, 0)]


def flipped(array, parts, bit):
    return lax.ppermute(array, "fsdp", [(spot, spot ^ bit) for spot in range(parts)])


def rounded_sum(terms):
    total = terms[0].astype(F32)
    for term in terms[1:]:
        total = total + term.astype(F32)
    return total.astype(BF16)


def reduced(keep, send, parts, place, steps):
    rows = keep.shape[0] // 8
    shape = (2, 2, 2, rows, keep.shape[1])
    terms = [keep.reshape(shape), flipped(send, parts, 1).reshape(shape)]
    for step in steps:
        if step == "seq":
            width = terms[0].shape[4] // 2
            away = [lax.dynamic_slice_in_dim(term, (1 - place) * width, width, 4) for term in terms]
            terms = [lax.dynamic_slice_in_dim(term, place * width, width, 4) for term in terms]
            came = lax.ppermute(rounded_sum(away), "seq", SWAP)
        else:
            axis = {8: 0, 4: 1, 2: 2}[step]
            away = [lax.slice_in_dim(term, 1, 2, axis=axis) for term in terms]
            terms = [lax.slice_in_dim(term, 0, 1, axis=axis) for term in terms]
            came = flipped(rounded_sum(away), parts, step)
        terms.append(came)
    return rounded_sum(terms).reshape(rows, -1)


def sides(mine, place):
    pair = jnp.stack([mine, lax.ppermute(mine, "seq", SWAP)])
    return jnp.where(place == 0, pair, pair[::-1])


def body(block_input, lead_gain, joint_weight, output_weight, tail_gain, up_weight, down_weight, cotangent):
    rows, triple = joint_weight.shape
    dim = block_input.shape[2]
    wide = up_weight.shape[1]
    half = block_input.shape[1]
    length = 2 * half
    parts = dim // rows
    group = triple // 6
    place = lax.axis_index("seq")
    me = lax.axis_index("fsdp")
    direct = parts == 16
    base = me if direct else jnp.zeros_like(me)
    spots = jnp.arange(16, dtype=jnp.int32)
    order = base ^ ((spots % 8) * 2 + spots // 8)
    few = jnp.arange(8, dtype=jnp.int32)
    inner_order = (base % 8) ^ ((few % 4) * 2 + few // 4)
    eight = (few % 2) * 8 + (few // 2 % 2) * 4 + few // 4 * 2
    arrived = base ^ jnp.concatenate([eight, eight ^ 1]) if direct else spots
    meta = jnp.concatenate([place[None], order, inner_order, (base // 8)[None], arrived]).astype(jnp.int32)

    joint_own = lax.dynamic_index_in_dim(joint_weight.reshape(rows, 3, 2, group), place, 2, keepdims=False)
    joint_own = joint_own.reshape(rows, 3, 3, PAIR).transpose(2, 0, 1, 3).reshape(3, rows, 3 * PAIR)
    up_turned = up_weight.reshape(rows, parts, 4, rows).transpose(0, 2, 1, 3).reshape(rows, wide)
    down_turned = down_weight.reshape(4, rows, dim).transpose(1, 0, 2).reshape(rows, 4 * dim)
    rest_shard = jnp.concatenate([output_weight, up_turned, down_turned], axis=1)

    own = block_input[0]
    upstream = cotangent[0]
    rest = lax.all_gather(rest_shard, "fsdp", axis=0, tiled=True)
    both_gains = jnp.stack([lead_gain, tail_gain])
    if direct:
        gains = lax.dynamic_update_slice(jnp.zeros((2, dim), BF16), both_gains, (0, me * rows))
        for bit in (1, 2, 4, 8):
            gains = gains + flipped(gains, parts, bit)
    else:
        gains = lax.all_gather(both_gains, "fsdp", axis=1, tiled=True)
    other = lax.ppermute(own, "seq", SWAP)
    firsts = []
    for pair in range(3):
        block = joint_own[pair]
        if direct:
            for bit in (8, 4, 2):
                block = jnp.concatenate([block, flipped(block, parts, bit)], axis=0)
            firsts.append((block, flipped(block, parts, 1)))
        else:
            block = lax.all_gather(block, "fsdp", axis=0, tiled=True)
            firsts.append((block[: dim // 2], block[dim // 2 :]))

    zb, zt = call(
        first_norm, "first_norm", (shaped(length, dim), shaped(dim, length)), 3, [pltpu.VMEM((dim, length), BF16)]
    )(meta, own, other, gains)

    kept = []
    received = []
    for pair in range(3):
        qkv, o_own, o_other, lse, weight = call(
            attend,
            "attend",
            (
                shaped(length, 3 * PAIR),
                shaped(half, PAIR),
                shaped(half, PAIR),
                shaped(8, length, dtype=F32),
                shaped(dim, 3 * PAIR),
            ),
            3,
            [
                pltpu.VMEM((2, length, PAIR), BF16),
                pltpu.VMEM((PAIR, length), BF16),
                pltpu.VMEM((length, BAND), F32),
                pltpu.VMEM((length, BAND), BF16),
                pltpu.VMEM((PAIR, BAND), F32),
                pltpu.VMEM((length, PAIR), BF16),
            ],
            took=8,
        )(meta, zb, *firsts[pair])
        kept.append((qkv, o_own, o_other, lse, weight))
        received.append(lax.ppermute(o_other, "seq", SWAP))

    rest_block = pl.BlockSpec((dim, dim), lambda *_: (0, 0))
    resid, zb_two, zt_two, mixed_t = pl.pallas_call(
        project_out,
        name="project_out",
        grid=(1,),
        out_shape=(shaped(half, dim, dtype=F32), shaped(half, dim), shaped(dim, half), shaped(dim, half)),
        in_specs=[SMEM] + [VMEM] * 8 + [rest_block],
        out_specs=[VMEM] * 4,
        cost_estimate=cost(5),
        scratch_shapes=[pltpu.VMEM((half, dim), BF16), pltpu.VMEM((dim, half), BF16)],
        compiler_params=pltpu.CompilerParams(vmem_limit_bytes=LIMIT),
    )(meta, own, *[k[1] for k in kept], *received, gains, rest)

    chunk = dim // 2
    steps = wide // chunk
    whole = lambda *dims: pl.BlockSpec(dims, lambda *_: (0,) * len(dims))
    out, g_two, up_keep, up_send, down_keep, down_send = pl.pallas_call(
        feed,
        name="feed",
        out_shape=(
            shaped(half, dim),
            shaped(half, dim, dtype=F32),
            shaped(dim // 2, wide),
            shaped(dim // 2, wide),
            shaped(2, dim // 4, 4 * dim),
            shaped(2, dim // 4, 4 * dim),
        ),
        grid_spec=pltpu.PrefetchScalarGridSpec(
            num_scalar_prefetch=1,
            grid=(steps,),
            in_specs=[
                whole(half, dim),
                whole(dim, half),
                pl.BlockSpec((dim, chunk), lambda m, meta: (0, 2 + m // 2 * 2 + (m % 2) ^ meta[25])),
                pl.BlockSpec((chunk, dim), lambda m, meta: ((m % 2) ^ meta[25], 5 + m // 2)),
                whole(half, dim),
                whole(half, dim),
            ],
            out_specs=[
                whole(half, dim),
                whole(half, dim),
                pl.BlockSpec((dim // 2, chunk), lambda m, meta: (0, m // 2 * 2 + (m % 2) ^ meta[25])),
                pl.BlockSpec((dim // 2, chunk), lambda m, meta: (0, m // 2 * 2 + (m % 2) ^ meta[25])),
                pl.BlockSpec((1, dim // 4, dim), lambda m, meta: (m % 2, 0, m // 2)),
                pl.BlockSpec((1, dim // 4, dim), lambda m, meta: (m % 2, 0, m // 2)),
            ],
            scratch_shapes=[
                pltpu.VMEM((half, dim), F32),
                pltpu.VMEM((half, dim), F32),
                pltpu.VMEM((chunk, half), BF16),
                pltpu.VMEM((chunk, half), BF16),
            ],
        ),
        compiler_params=pltpu.CompilerParams(vmem_limit_bytes=LIMIT, dimension_semantics=("arbitrary",)),
        cost_estimate=cost(29),
    )(meta, zb_two, zt_two, rest, rest, upstream, resid)

    dresid, db, *dm = pl.pallas_call(
        branch_back,
        name="branch_back",
        grid=(1,),
        out_shape=(shaped(half, dim, dtype=F32), shaped(half, dim)) + (shaped(half, PAIR),) * 6,
        in_specs=[SMEM] + [VMEM] * 4 + [rest_block],
        out_specs=[VMEM] * 8,
        compiler_params=pltpu.CompilerParams(vmem_limit_bytes=LIMIT),
        cost_estimate=cost(5),
    )(meta, g_two, resid, upstream, gains, rest)
    incoming = [lax.ppermute(part, "seq", SWAP) for part in dm[:3]]
    halves = (shaped(dim // 2, dim), shaped(dim // 2, dim))
    output_keep, output_send = call(output_back, "output_back", halves, 2)(meta, mixed_t, db)

    token_own = []
    token_other = []
    joint_parts = []
    for pair in range(3):
        qkv, o_own, o_other, lse, weight = kept[pair]
        g_own, g_other, keep, send = call(
            attend_back,
            "attend_back",
            (
                shaped(half, 3 * PAIR),
                shaped(half, 3 * PAIR),
                shaped(dim // 2, 3 * PAIR),
                shaped(dim // 2, 3 * PAIR),
            ),
            7,
            [
                pltpu.VMEM((2, length, PAIR), BF16),
                pltpu.VMEM((2, length, PAIR), BF16),
                pltpu.VMEM((PAIR, length), BF16),
                pltpu.VMEM((length, PAIR), BF16),
                pltpu.VMEM((8, length), F32),
                pltpu.VMEM((length, PAIR), F32),
                pltpu.VMEM((length, PAIR), F32),
                pltpu.VMEM((PAIR, BAND), F32),
                pltpu.VMEM((length, 3 * PAIR), BF16),
            ],
            took=9,
        )(meta, qkv, o_own, o_other, dm[3 + pair], incoming[pair], lse, zt)
        token_own.append(g_own)
        token_other.append(g_other)
        joint_parts.append((keep, send))

    weights = [k[4] for k in kept]
    (sent,) = call(token_back, "token_back", (shaped(half, dim),), 6)(meta, *token_other, *weights)
    other_part = lax.ppermute(sent, "seq", SWAP)
    (own_part,) = call(token_back, "token_back_own", (shaped(half, dim, dtype=F32),), 6)(meta, *token_own, *weights)
    (input_grad,) = call(input_back, "input_back", (shaped(half, dim, dtype=F32),), 5)(
        meta, own, own_part, other_part, dresid, gains
    )

    down_keep, down_send = (part.reshape(dim // 2, 4 * dim) for part in (down_keep, down_send))

    if direct:
        up_sum, down_sum, output_sum = (
            sides(reduced(keep, send, parts, place, steps), place).transpose(1, 0, 2).reshape(rows, -1).astype(F32)
            for keep, send, steps in (
                (up_keep, up_send, (2, "seq", 4, 8)),
                (down_keep, down_send, ("seq", 4, 2, 8)),
                (output_keep, output_send, (4, 2, "seq", 8)),
            )
        )
        joint_mine = jnp.stack(
            [reduced(keep, send, parts, place, (2, 4, 8)) for keep, send in joint_parts]
        )
    else:

        def scattered(keep, send):
            part = jnp.stack([keep, send]).reshape(2, 8, dim // 16, -1).transpose(1, 0, 2, 3).reshape(dim, -1)
            return lax.psum_scatter(part, "fsdp", scatter_dimension=0, tiled=True)

        up_sum, down_sum, output_sum = (
            lax.psum(scattered(keep, send), "seq").astype(F32)
            for keep, send in ((up_keep, up_send), (down_keep, down_send), (output_keep, output_send))
        )
        joint_mine = jnp.stack([scattered(keep, send) for keep, send in joint_parts])
    joint_sides = sides(joint_mine, place).astype(F32)
    joint_grad = joint_sides.reshape(2, 3, rows, 3, PAIR).transpose(2, 3, 0, 1, 4).reshape(rows, triple)
    lead_grad = jnp.sum(joint_grad * joint_weight.astype(F32), axis=1) / lead_gain.astype(F32)
    up_grad = up_sum.reshape(rows, 4, parts, rows).transpose(0, 2, 1, 3).reshape(rows, wide)
    tail_grad = jnp.sum(up_grad * up_weight.astype(F32), axis=1) / tail_gain.astype(F32)
    down_grad = down_sum.reshape(rows, 4, dim).transpose(1, 0, 2).reshape(4 * rows, dim)
    return (out[None], input_grad[None], lead_grad, joint_grad, output_sum, tail_grad, up_grad, down_grad)


def solution(mesh):
    split = P("fsdp", "seq", None)
    placed = (split, P("fsdp"), P("fsdp", None), P("fsdp", None), P("fsdp"), P("fsdp", None), P("fsdp", None), split)
    return jax.shard_map(
        body,
        mesh=mesh,
        in_specs=placed,
        out_specs=(split, split, P("fsdp"), P("fsdp", None), P("fsdp", None), P("fsdp"), P("fsdp", None), P("fsdp", None)),
        check_vma=False,
    )
```

time: 767 us -> 343 us (0.45)
  waiting for transfers between devices: 369 us -> 118 us
  matrix products: 121 us -> 0 us
  Pallas kernels: 0 us -> 111 us
  blocking collectives: 111 us -> 0 us
  other arithmetic: 71.7 us -> 17.7 us
  starting transfers between devices: 13.2 us -> 51 us
  local copies, waits for them, and re-layouts: 56.6 us -> 26.8 us
    reduce_scatter x4 -> x0, waiting for transfers between devices: 281 us -> none  [the longest x1 114 us: body(): lax.psum_scatter(up_part, 'fsdp', scatter_dimension=0, tiled=True)]
    dot_general x24 -> x0, matrix products: 121 us -> none  [the longest x4 28.1 us: outer_sum(): lax.dot_general(left, right, (((0,), (0,)), ((), ())), preferred_element_...]
    pallas_call x0 -> x14, Pallas kernels: none -> 111 us  [the longest x1 29.5 us: body(): pl.pallas_call(feed, name='feed', out_shape=(shaped(half, dim), shaped(ha...]
    ppermute x0 -> x55, waiting for transfers between devices: none -> 105 us  [the longest x40 84.5 us: flipped(): lax.ppermute(array, 'fsdp', [(spot, spot ^ bit) for spot in range(parts)])]
    unnamed x2 -> x0, blocking collectives: 67.9 us -> none
    ppermute x0 -> x55, starting transfers between devices: none -> 50.9 us  [the longest x40 33.3 us: flipped(): lax.ppermute(array, 'fsdp', [(spot, spot ^ bit) for spot in range(parts)])]
    all_to_all x3 -> x0, waiting for transfers between devices: 44.8 us -> none  [the longest x1 26.4 us: body(): lax.all_to_all(projected.reshape(tokens, 3, groups, width), 'seq', split_...]
    all_to_all x1 -> x0, blocking collectives: 38.3 us -> none  [body(): lax.all_to_all(stacked.reshape(length, 3, 1, width), 'seq', split_axis=0,...]
  transfers between devices with their start and end apart: 12 -> 56, of which waited for: 8 -> 28; matrix products, arithmetic and copies ran while one was open for 29% -> 9% of each run, Pallas kernels for 0% -> 23%
where the time goes in v1:
time: 343 us; the launch traced here: 339 us
  waiting for transfers between devices  118 us (34%)
  Pallas kernels  111 us (32%)
  starting transfers between devices  51 us (15%)
  local copies, waits for them, and re-layouts  26.8 us (8%)
  other arithmetic  17.7 us (5%)
  between operations  15.3 us (4%)
    ppermute x40, waiting for transfers between devices, flipped(): lax.ppermute(array, 'fsdp', [(spot, spot ^ bit) for spot in range(parts)])  84.5 us
    ppermute x40, starting transfers between devices, flipped(): lax.ppermute(array, 'fsdp', [(spot, spot ^ bit) for spot in range(parts)])  33.3 us
    pallas_call x1, Pallas kernels, body(): pl.pallas_call(feed, name='feed', out_shape=(shaped(half, dim), shaped(ha...  29.5 us
    pallas_call x3, Pallas kernels, body(): call(attend_back, 'attend_back', (shaped(half, 3 * PAIR), shaped(half, 3...  27.3 us
    pallas_call x3, Pallas kernels, body(): call(attend, 'attend', (shaped(length, 3 * PAIR), shaped(half, PAIR), sha...  23 us
    all_gather x1, waiting for transfers between devices, body(): rest = lax.all_gather(rest_shard, 'fsdp', axis=0, tiled=True)  12.8 us
    convert_element_type x24, other arithmetic, rounded_sum(): return total.astype(BF16)  12.1 us
    ppermute x3, waiting for transfers between devices, reduced(): came = lax.ppermute(rounded_sum(away), 'seq', SWAP)  10.9 us
  transfers between devices with their start and end apart: 56, of which 28 were waited for; matrix products, arithmetic and copies ran while one was open for 9% of the time, Pallas kernels for 23%

profile of v1, /device:TPU:0, one launch (start us, length us, event | category | flops | bytes accessed | tf_op | source)
XLA Modules:
  0.0 339.1 jit_solution(14368893671131211538)
XLA Ops:
  12.6 2.5 collective-permute-start
  15.7 2.7 collective-permute-start.13
  18.9 2.7 collective-permute-start.5
  27.5 2.1 collective-permute-done.3
  30.4 3.9 %collective-permute-done.4 = bf16[2,768]{1,0:T(2,128)(2,1)S(1)} collective-permute-done((bf16[2,768]{1,0:T(2,128)(2,1)S(1)}, bf16[2,768]{1,0:T(2,128)(2,1)S(1)}, u32[]{:S(2)}, u32[]{:S(2)}) %collective-permute-start.4) | collective-permute-done | bytes 3104 | tf_op jit(solution)/shard_map/ppermute | solution.py:289
  38.7 4.8 %collective-permute-done.14 = bf16[96,384]{1,0:T(8,128)(2,1)S(1)} collective-permute-done((bf16[96,384]{1,0:T(8,128)(2,1)S(1)}, bf16[96,384]{1,0:T(8,128)(2,1)S(1)}, u32[]{:S(2)}, u32[]{:S(2)}) %collective-permute-start.14) | collective-permute-done | bytes 73760 | tf_op jit(solution)/shard_map/ppermute | solution.py:289
  45.1 2.9 collective-permute-done.10
  49.5 2.1 collective-permute-done.6
  54.0 2.8 collective-permute-done.7
  57.9 4.8 %first_norm.1 = (bf16[1024,768]{1,0:T(8,128)(2,1)}, bf16[768,1024]{1,0:T(8,128)(2,1)}) custom-call(s32[42]{0:T(128)} %concatenate.43.meta, bf16[512,768]{1,0:T(8,128)(2,1)} %bitcast.151, bf16[512,768]{1,0:T(8,128)(2,1)} %copy-done.23, bf16[2,768]{1,0:T(2,128)(2,1)} %add.332.gains), custom_call_target="tpu_custom_call" | custom-call | flops 4000000000 | bytes 12000000 | tf_op jit(solution)/shard_map/first_norm/pallas_call | solution.py:371
  63.4 7.5 %attend.5 = (bf16[1024,384]{1,0:T(8,128)(2,1)}, bf16[512,128]{1,0:T(8,128)(2,1)}, bf16[512,128]{1,0:T(8,128)(2,1)}, f32[8,1024]{1,0:T(8,128)}, bf16[768,384]{1,0:T(8,128)(2,1)}) custom-call(s32[42]{0:T(128)} %concatenate.43.meta, bf16[1024,768]{1,0:T(8,128)(2,1)} %get-tuple-element.57.zb, bf16[384,384]{1,0:T(8,128)(2,1)} %copy-done.17, ...), custom_call_target="tpu_custom_call" | custom-call | flops 8000000000 | bytes 24000000 | tf_op jit(solution)/shard_map/attend/pallas_call | solution.py:378
  72.6 7.5 %attend.4 = (bf16[1024,384]{1,0:T(8,128)(2,1)}, bf16[512,128]{1,0:T(8,128)(2,1)}, bf16[512,128]{1,0:T(8,128)(2,1)}, f32[8,1024]{1,0:T(8,128)}, bf16[768,384]{1,0:T(8,128)(2,1)}) custom-call(s32[42]{0:T(128)} %concatenate.43.meta, bf16[1024,768]{1,0:T(8,128)(2,1)} %get-tuple-element.57.zb, bf16[384,384]{1,0:T(8,128)(2,1)} %copy-done.18, ...), custom_call_target="tpu_custom_call" | custom-call | flops 8000000000 | bytes 24000000 | tf_op jit(solution)/shard_map/attend/pallas_call | solution.py:378
  81.9 8.0 %attend.3 = (bf16[1024,384]{1,0:T(8,128)(2,1)}, bf16[512,128]{1,0:T(8,128)(2,1)}, bf16[512,128]{1,0:T(8,128)(2,1)}, f32[8,1024]{1,0:T(8,128)}, bf16[768,384]{1,0:T(8,128)(2,1)}) custom-call(s32[42]{0:T(128)} %concatenate.43.meta, bf16[1024,768]{1,0:T(8,128)(2,1)} %get-tuple-element.57.zb, bf16[384,384]{1,0:T(8,128)(2,1)} %copy-done.19, ...), custom_call_target="tpu_custom_call" | custom-call | flops 8000000000 | bytes 24000000 | tf_op jit(solution)/shard_map/attend/pallas_call | solution.py:378
  90.8 4.5 %collective-permute-done.17.r0 = bf16[512,128]{1,0:T(8,128)(2,1)S(1)} collective-permute-done((bf16[512,128]{1,0:T(8,128)(2,1)}, bf16[512,128]{1,0:T(8,128)(2,1)S(1)}, u32[]{:S(2)}, u32[]{:S(2)}) %collective-permute-start.17) | collective-permute-done | bytes 131104 | tf_op jit(solution)/shard_map/ppermute | solution.py:400
  95.3 12.8 %all-gather.2.cloned.1.call-done.weight.up.down = bf16[768,6912]{1,0:T(8,128)(2,1)} async-done(((bf16[48,6912]{1,0:T(8,128)(2,1)}), bf16[768,6912]{1,0:T(8,128)(2,1)}) %all-gather.2.cloned.1.call-update) | async-done | bytes 10616848 | tf_op jit(solution)/shard_map/all_gather | solution.py:351
  108.1 4.8 %project_out.1 = (f32[512,768]{1,0:T(8,128)}, bf16[512,768]{1,0:T(8,128)(2,1)}, bf16[768,512]{1,0:T(8,128)(2,1)}, bf16[768,512]{1,0:T(8,128)(2,1)}) custom-call(s32[42]{0:T(128)} %concatenate.43.meta, bf16[512,768]{1,0:T(8,128)(2,1)} %bitcast.152, bf16[512,128]{1,0:T(8,128)(2,1)} %get-tuple-element.58.o0.o_own, bf16[512,128]{1,0:T(8,128)(2,1)} %get-tuple-element.59.o1.o_own, ...), custom_call_target="tpu_custom_call" | custom-call | flops 5000000000 | bytes 15000000 | tf_op jit(solution)/shard_map/project_out/pallas_call | solution.py:403
  112.9 29.5 %feed.1 = (bf16[512,768]{1,0:T(8,128)(2,1)}, f32[512,768]{1,0:T(8,128)}, bf16[384,3072]{1,0:T(8,128)(2,1)}, bf16[384,3072]{1,0:T(8,128)(2,1)}, bf16[2,192,3072]{...) custom-call(s32[42]{0:T(128)} %concatenate.43.meta, bf16[512,768]{1,0:T(8,128)(2,1)} %get-tuple-element.64.zb, ...), custom_call_target="tpu_custom_call" | custom-call | flops 28999999488 | bytes 87000000 | tf_op jit(solution)/shard_map/feed/pallas_call | solution.py:418
  142.9 5.3 %branch_back.1 = (f32[512,768]{1,0:T(8,128)}, bf16[512,768]{1,0:T(8,128)(2,1)}, bf16[512,128]{1,0:T(8,128)(2,1)}, bf16[512,128]{1,0:T(8,128)(2,1)}, bf16[512,128...) custom-call(s32[42]{0:T(128)} %concatenate.43.meta, ...), custom_call_target="tpu_custom_call" | custom-call | flops 5000000000 | bytes 15000000 | tf_op jit(solution)/shard_map/branch_back/pallas_call | solution.py:459
  149.6 3.1 output_back.1
  156.6 9.0 %attend_back.3 = (bf16[512,384]{1,0:T(8,128)(2,1)}, bf16[512,384]{1,0:T(8,128)(2,1)}, bf16[384,384]{1,0:T(8,128)(2,1)}, bf16[384,384]{1,0:T(8,128)(2,1)}) custom-call(s32[42]{0:T(128)} %concatenate.43.meta, bf16[1024,384]{1,0:T(8,128)(2,1)} %get-tuple-element.68.qkv, bf16[512,128]{1,0:T(8,128)(2,1)} %get-tuple-element.58.o0.o_own, ...), custom_call_target="tpu_custom_call" | custom-call | flops 8999999488 | bytes 27000000 | tf_op jit(solution)/shard_map/attend_back/pallas_call | solution.py:478
  166.3 9.2 %attend_back.4 = (bf16[512,384]{1,0:T(8,128)(2,1)}, bf16[512,384]{1,0:T(8,128)(2,1)}, bf16[384,384]{1,0:T(8,128)(2,1)}, bf16[384,384]{1,0:T(8,128)(2,1)}) custom-call(s32[42]{0:T(128)} %concatenate.43.meta, bf16[1024,384]{1,0:T(8,128)(2,1)} %get-tuple-element.75.qkv, bf16[512,128]{1,0:T(8,128)(2,1)} %get-tuple-element.59.o1.o_own, ...), custom_call_target="tpu_custom_call" | custom-call | flops 8999999488 | bytes 27000000 | tf_op jit(solution)/shard_map/attend_back/pallas_call | solution.py:478
  176.2 9.0 %attend_back.5 = (bf16[512,384]{1,0:T(8,128)(2,1)}, bf16[512,384]{1,0:T(8,128)(2,1)}, bf16[384,384]{1,0:T(8,128)(2,1)}, bf16[384,384]{1,0:T(8,128)(2,1)}) custom-call(s32[42]{0:T(128)} %concatenate.43.meta, bf16[1024,384]{1,0:T(8,128)(2,1)} %get-tuple-element.80.qkv, bf16[512,128]{1,0:T(8,128)(2,1)} %get-tuple-element.60.o2.o_own, ...), custom_call_target="tpu_custom_call" | custom-call | flops 8999999488 | bytes 27000000 | tf_op jit(solution)/shard_map/attend_back/pallas_call | solution.py:478
  185.3 4.1 %token_back.1 = bf16[512,768]{1,0:T(8,128)(2,1)} custom-call(s32[42]{0:T(128)} %concatenate.43.meta, bf16[512,384]{1,0:T(8,128)(2,1)} %get-tuple-element.88.g0, bf16[512,384]{1,0:T(8,128)(2,1)} %get-tuple-element.89.g1, bf16[512,384]{1,0:T(8,128)(2,1)} %get-tuple-element.90.g2, bf16[768,384]{1,0:T(8,128)(2,1)} %get-tuple-element.85.w0, ...), custom_call_target="tpu_custom_call" | custom-call | flops 4000000000 | bytes 12000000 | tf_op jit(solution)/shard_map/token_back/pallas_call | solution.py:506
  189.3 4.4 %token_back_own.1.mine = f32[512,768]{1,0:T(8,128)} custom-call(s32[42]{0:T(128)} %concatenate.43.meta, bf16[512,384]{1,0:T(8,128)(2,1)} %get-tuple-element.74.g0, bf16[512,384]{1,0:T(8,128)(2,1)} %get-tuple-element.79.g1, bf16[512,384]{1,0:T(8,128)(2,1)} %get-tuple-element.84.g2, bf16[768,384]{1,0:T(8,128)(2,1)} %get-tuple-element.85.w0, ...), custom_call_target="tpu_custom_call" | custom-call | flops 4000000000 | bytes 12000000 | tf_op jit(solution)/shard_map/token_back_own/pallas_call | solution.py:508
  196.0 5.3 %collective-permute-done.25 = bf16[2,2,1,48,384]{4,3,2,1,0:T(8,128)(2,1)S(1)} collective-permute-done((bf16[2,2,1,48,384]{4,3,2,1,0:T(8,128)(2,1)S(1)}, bf16[2,2,1,48,384]{4,3,2,1,0:T(8,128)(2,1)S(1)}, u32[]{:S(2)}, u32[]{:S(2)}) %collective-permute-start.25) | collective-permute-done | bytes 147488 | tf_op jit(solution)/shard_map/ppermute | solution.py:289
  201.9 4.6 %collective-permute-done.29 = bf16[2,2,1,48,384]{4,3,2,1,0:T(8,128)(2,1)S(1)} collective-permute-done((bf16[2,2,1,48,384]{4,3,2,1,0:T(8,128)(2,1)S(1)}, bf16[2,2,1,48,384]{4,3,2,1,0:T(8,128)(2,1)S(1)}, u32[]{:S(2)}, u32[]{:S(2)}) %collective-permute-start.29) | collective-permute-done | bytes 147488 | tf_op jit(solution)/shard_map/ppermute | solution.py:289
  207.1 4.5 %collective-permute-done.33 = bf16[2,2,1,48,384]{4,3,2,1,0:T(8,128)(2,1)S(1)} collective-permute-done((bf16[2,2,1,48,384]{4,3,2,1,0:T(8,128)(2,1)S(1)}, bf16[2,2,1,48,384]{4,3,2,1,0:T(8,128)(2,1)S(1)}, u32[]{:S(2)}, u32[]{:S(2)}) %collective-permute-start.33) | collective-permute-done | bytes 147488 | tf_op jit(solution)/shard_map/ppermute | solution.py:289
  212.1 4.2 %collective-permute-done.26 = bf16[2,1,1,48,384]{4,3,2,1,0:T(8,128)(2,1)S(1)} collective-permute-done((bf16[2,1,1,48,384]{4,3,2,1,0:T(8,128)(2,1)S(1)}, bf16[2,1,1,48,384]{4,3,2,1,0:T(8,128)(2,1)S(1)}, u32[]{:S(2)}, u32[]{:S(2)}) %collective-permute-start.26) | collective-permute-done | bytes 73760 | tf_op jit(solution)/shard_map/ppermute | solution.py:289
  216.8 3.9 %collective-permute-done.30 = bf16[2,1,1,48,384]{4,3,2,1,0:T(8,128)(2,1)S(1)} collective-permute-done((bf16[2,1,1,48,384]{4,3,2,1,0:T(8,128)(2,1)S(1)}, bf16[2,1,1,48,384]{4,3,2,1,0:T(8,128)(2,1)S(1)}, u32[]{:S(2)}, u32[]{:S(2)}) %collective-permute-start.30) | collective-permute-done | bytes 73760 | tf_op jit(solution)/shard_map/ppermute | solution.py:289
  221.3 3.9 %collective-permute-done.34 = bf16[2,1,1,48,384]{4,3,2,1,0:T(8,128)(2,1)S(1)} collective-permute-done((bf16[2,1,1,48,384]{4,3,2,1,0:T(8,128)(2,1)S(1)}, bf16[2,1,1,48,384]{4,3,2,1,0:T(8,128)(2,1)S(1)}, u32[]{:S(2)}, u32[]{:S(2)}) %collective-permute-start.34) | collective-permute-done | bytes 73760 | tf_op jit(solution)/shard_map/ppermute | solution.py:289
  226.7 3.6 %collective-permute-done.27 = bf16[1,1,1,48,384]{4,3,2,1,0:T(8,128)(2,1)S(1)} collective-permute-done((bf16[1,1,1,48,384]{4,3,2,1,0:T(8,128)(2,1)S(1)}, bf16[1,1,1,48,384]{4,3,2,1,0:T(8,128)(2,1)S(1)}, u32[]{:S(2)}, u32[]{:S(2)}) %collective-permute-start.27) | collective-permute-done | bytes 36896 | tf_op jit(solution)/shard_map/ppermute | solution.py:289
  231.5 3.6 %collective-permute-done.31 = bf16[1,1,1,48,384]{4,3,2,1,0:T(8,128)(2,1)S(1)} collective-permute-done((bf16[1,1,1,48,384]{4,3,2,1,0:T(8,128)(2,1)S(1)}, bf16[1,1,1,48,384]{4,3,2,1,0:T(8,128)(2,1)S(1)}, u32[]{:S(2)}, u32[]{:S(2)}) %collective-permute-start.31) | collective-permute-done | bytes 36896 | tf_op jit(solution)/shard_map/ppermute | solution.py:289
  236.4 4.0 %collective-permute-done.35 = bf16[1,1,1,48,384]{4,3,2,1,0:T(8,128)(2,1)S(1)} collective-permute-done((bf16[1,1,1,48,384]{4,3,2,1,0:T(8,128)(2,1)S(1)}, bf16[1,1,1,48,384]{4,3,2,1,0:T(8,128)(2,1)S(1)}, u32[]{:S(2)}, u32[]{:S(2)}) %collective-permute-start.35) | collective-permute-done | bytes 36896 | tf_op jit(solution)/shard_map/ppermute | solution.py:289
  243.4 2.1 collective-permute-done.36
  246.3 2.0 reshape.161
  248.3 2.2 copy.36
  250.5 2.1 reshape.151
  257.0 4.7 %collective-permute-done.39 = bf16[2,1,1,48,768]{4,3,2,1,0:T(8,128)(2,1)S(1)} collective-permute-done((bf16[2,1,1,48,768]{4,3,2,1,0:T(8,128)(2,1)S(1)}, bf16[2,1,1,48,768]{4,3,2,1,0:T(8,128)(2,1)S(1)}, u32[]{:S(2)}, u32[]{:S(2)}) %collective-permute-start.39) | collective-permute-done | bytes 147488 | tf_op jit(solution)/shard_map/ppermute | solution.py:289
  262.6 2.1 add_convert_fusion
  270.1 2.0 collective-permute-done.41
  272.9 9.9 %collective-permute-done.50 = bf16[2,2,2,48,1536]{4,3,2,1,0:T(8,128)(2,1)S(1)} collective-permute-done((bf16[2,2,2,48,1536]{4,3,2,1,0:T(8,128)(2,1)S(1)}, bf16[2,2,2,48,1536]{4,3,2,1,0:T(8,128)(2,1)S(1)}, u32[]{:S(2)}, u32[]{:S(2)}) %collective-permute-start.50) | collective-permute-done | bytes 1179680 | tf_op jit(solution)/shard_map/ppermute | solution.py:308
  283.8 2.1 add_convert_fusion.2
  286.1 4.5 %input_back.1 = f32[512,768]{1,0:T(8,128)} custom-call(s32[42]{0:T(128)} %concatenate.43.meta, bf16[512,768]{1,0:T(8,128)(2,1)} %bitcast.153, f32[512,768]{1,0:T(8,128)} %token_back_own.1.mine, bf16[512,768]{1,0:T(8,128)(2,1)} %collective-permute-done.23.other, f32[512,768]{1,0:T(8,128)} %get-tuple-element.91.dresid, bf16[2,768]{1,0:T(2,128)(2,1)} %add.332.gains), custom_call_target="tpu_custom_call" | custom-call | flops 4000000000 | bytes 12000000 | tf_op jit(solution)/shard_map/input_back/pallas_call | solution.py:509
  293.4 7.4 %collective-permute-done.51 = bf16[2,1,2,48,1536]{4,3,2,1,0:T(8,128)(2,1)} collective-permute-done((bf16[2,1,2,48,1536]{4,3,2,1,0:T(8,128)(2,1)}, bf16[2,1,2,48,1536]{4,3,2,1,0:T(8,128)(2,1)}, u32[]{:S(2)}, u32[]{:S(2)}) %collective-permute-start.51) | collective-permute-done | bytes 589856 | tf_op jit(solution)/shard_map/ppermute | solution.py:289
  303.1 5.7 %collective-permute-done.52 = bf16[2,1,1,48,1536]{4,3,2,1,0:T(8,128)(2,1)S(1)} collective-permute-done((bf16[2,1,1,48,1536]{4,3,2,1,0:T(8,128)(2,1)S(1)}, bf16[2,1,1,48,1536]{4,3,2,1,0:T(8,128)(2,1)S(1)}, u32[]{:S(2)}, u32[]{:S(2)}) %collective-permute-start.52) | collective-permute-done | bytes 294944 | tf_op jit(solution)/shard_map/ppermute | solution.py:289
  310.1 3.0 collective-permute-start.47
  313.1 5.6 %collective-permute-done.53 = bf16[1,1,1,48,1536]{4,3,2,1,0:T(8,128)(2,1)S(1)} collective-permute-done((bf16[1,1,1,48,1536]{4,3,2,1,0:T(8,128)(2,1)S(1)}, bf16[1,1,1,48,1536]{4,3,2,1,0:T(8,128)(2,1)S(1)}, u32[]{:S(2)}, u32[]{:S(2)}) %collective-permute-start.53) | collective-permute-done | bytes 147488 | tf_op jit(solution)/shard_map/ppermute | solution.py:289
  322.2 2.7 collective-permute-done.54
  (252 shorter events, 78.2 us)
Async XLA Ops:
  7.2 100.9 %all-gather.2.cloned.1.call-start = ((), (), s32[]{:S(2)}) async-start(), calls=%async_computation | async-start | bytes 11280384 | tf_op jit(solution)/shard_map/all_gather | solution.py:351
  12.0 9.6 %collective-permute-start.1 = (bf16[2,768]{1,0:T(2,128)(2,1)S(1)}, bf16[2,768]{1,0:T(2,128)(2,1)S(1)}, u32[]{:S(2)}, u32[]{:S(2)}) collective-permute-start(bf16[2,768]{1,0:T(2,128)(2,1)S(1)} %dynamic_update_slice.5), channel_id=1, source_target_pairs={{0,1},{1,0},{2,3},{3,2},{4,5},{5,4},{6,7},{7,6},{8,9},{9,8},{10,11... | collective-permute-start | bytes 9224 | tf_op jit(solution)/shard_map/ppermute | solution.py:289
  12.6 44.4 %collective-permute-start = (bf16[512,768]{1,0:T(8,128)(2,1)S(1)}, bf16[512,768]{1,0:T(8,128)(2,1)S(1)}, u32[]{:S(2)}, u32[]{:S(2)}) collective-permute-start(bf16[512,768]{1,0:T(8,128)(2,1)S(1)} %bitcast.154), channel_id=1, source_target_pairs={{0,16},{16,0},{1,17},{17,1},{2,18},{18,2},{3,19},{19,3},{4,20},{20... | collective-permute-start | bytes 2359304 | tf_op jit(solution)/shard_map/ppermute | solution.py:359
  15.7 19.2 %collective-permute-start.13 = (bf16[48,384]{1,0:T(8,128)(2,1)S(1)}, bf16[48,384]{1,0:T(8,128)(2,1)S(1)}, u32[]{:S(2)}, u32[]{:S(2)}) collective-permute-start(bf16[48,384]{1,0:T(8,128)(2,1)S(1)} %get-tuple-element.107), channel_id=1, source_target_pairs={{0,8},{1,9},{2,10},{3,11},{4,12},{5,13},{6,14},{7,15},{8,0},{9,1},... | collective-permute-start | bytes 110600 | tf_op jit(solution)/shard_map/ppermute | solution.py:289
  18.4 18.1 %collective-permute-start.9 = (bf16[48,384]{1,0:T(8,128)(2,1)S(1)}, bf16[48,384]{1,0:T(8,128)(2,1)S(1)}, u32[]{:S(2)}, u32[]{:S(2)}) collective-permute-start(bf16[48,384]{1,0:T(8,128)(2,1)S(1)} %get-tuple-element.109), channel_id=1, source_target_pairs={{0,8},{1,9},{2,10},{3,11},{4,12},{5,13},{6,14},{7,15},{8,0},{9,1},... | collective-permute-start | bytes 110600 | tf_op jit(solution)/shard_map/ppermute | solution.py:289
  18.9 18.2 %collective-permute-start.5 = (bf16[48,384]{1,0:T(8,128)(2,1)S(1)}, bf16[48,384]{1,0:T(8,128)(2,1)S(1)}, u32[]{:S(2)}, u32[]{:S(2)}) collective-permute-start(bf16[48,384]{1,0:T(8,128)(2,1)S(1)} %get-tuple-element.111), channel_id=1, source_target_pairs={{0,8},{1,9},{2,10},{3,11},{4,12},{5,13},{6,14},{7,15},{8,0},{9,1},... | collective-permute-start | bytes 110600 | tf_op jit(solution)/shard_map/ppermute | solution.py:289
  34.9 8.6 %collective-permute-start.14 = (bf16[96,384]{1,0:T(8,128)(2,1)S(1)}, bf16[96,384]{1,0:T(8,128)(2,1)S(1)}, u32[]{:S(2)}, u32[]{:S(2)}) collective-permute-start(bf16[96,384]{1,0:T(8,128)(2,1)S(1)} %pad_maximum_fusion.10), channel_id=1, source_target_pairs={{0,4},{1,5},{2,6},{3,7},{4,0},{5,1},{6,2},{7,3},{8,12},{9,13},{10,... | collective-permute-start | bytes 221192 | tf_op jit(solution)/shard_map/ppermute | solution.py:289
  36.5 11.5 %collective-permute-start.10 = (bf16[96,384]{1,0:T(8,128)(2,1)S(1)}, bf16[96,384]{1,0:T(8,128)(2,1)S(1)}, u32[]{:S(2)}, u32[]{:S(2)}) collective-permute-start(bf16[96,384]{1,0:T(8,128)(2,1)S(1)} %pad_maximum_fusion.9), channel_id=1, source_target_pairs={{0,4},{1,5},{2,6},{3,7},{4,0},{5,1},{6,2},{7,3},{8,12},{9,13},{10,... | collective-permute-start | bytes 221192 | tf_op jit(solution)/shard_map/ppermute | solution.py:289
  37.1 14.5 %collective-permute-start.6 = (bf16[96,384]{1,0:T(8,128)(2,1)S(1)}, bf16[96,384]{1,0:T(8,128)(2,1)S(1)}, u32[]{:S(2)}, u32[]{:S(2)}) collective-permute-start(bf16[96,384]{1,0:T(8,128)(2,1)S(1)} %pad_maximum_fusion.8), channel_id=1, source_target_pairs={{0,4},{1,5},{2,6},{3,7},{4,0},{5,1},{6,2},{7,3},{8,12},{9,13},{10,... | collective-permute-start | bytes 221192 | tf_op jit(solution)/shard_map/ppermute | solution.py:289
  43.5 9.7 %collective-permute-start.15 = (bf16[192,384]{1,0:T(8,128)(2,1)S(1)}, bf16[192,384]{1,0:T(8,128)(2,1)S(1)}, u32[]{:S(2)}, u32[]{:S(2)}) collective-permute-start(bf16[192,384]{1,0:T(8,128)(2,1)S(1)} %pad_maximum_fusion.6), channel_id=1, source_target_pairs={{0,2},{1,3},{2,0},{3,1},{4,6},{5,7},{6,4},{7,5},{8,10},{9,11},{10,... | collective-permute-start | bytes 442376 | tf_op jit(solution)/shard_map/ppermute | solution.py:289
  48.0 5.4 %collective-permute-start.11 = (bf16[192,384]{1,0:T(8,128)(2,1)S(1)}, bf16[192,384]{1,0:T(8,128)(2,1)S(1)}, u32[]{:S(2)}, u32[]{:S(2)}) collective-permute-start(bf16[192,384]{1,0:T(8,128)(2,1)S(1)} %pad_maximum_fusion.5), channel_id=1, source_target_pairs={{0,2},{1,3},{2,0},{3,1},{4,6},{5,7},{6,4},{7,5},{8,10},{9,11},{10,... | collective-permute-start | bytes 442376 | tf_op jit(solution)/shard_map/ppermute | solution.py:289
  51.6 5.2 %collective-permute-start.7 = (bf16[192,384]{1,0:T(8,128)(2,1)S(1)}, bf16[192,384]{1,0:T(8,128)(2,1)S(1)}, u32[]{:S(2)}, u32[]{:S(2)}) collective-permute-start(bf16[192,384]{1,0:T(8,128)(2,1)S(1)} %pad_maximum_fusion.4), channel_id=1, source_target_pairs={{0,2},{1,3},{2,0},{3,1},{4,6},{5,7},{6,4},{7,5},{8,10},{9,11},{10,... | collective-permute-start | bytes 442376 | tf_op jit(solution)/shard_map/ppermute | solution.py:289
  53.3 9.3 %collective-permute-start.16 = (bf16[384,384]{1,0:T(8,128)(2,1)S(1)}, bf16[384,384]{1,0:T(8,128)(2,1)S(1)}, u32[]{:S(2)}, u32[]{:S(2)}) collective-permute-start(bf16[384,384]{1,0:T(8,128)(2,1)S(1)} %constant_dynamic-update-slice_fusion.8.near), channel_id=1, source_target_pairs={{0,1},{1,0},{2,3},{3,2},{4,5},{5,4},{6,7},{7,6},{8,9},{9,8},{10,11... | collective-permute-start | bytes 884744 | tf_op jit(solution)/shard_map/ppermute | solution.py:289
  53.4 18.4 %collective-permute-start.12 = (bf16[384,384]{1,0:T(8,128)(2,1)S(1)}, bf16[384,384]{1,0:T(8,128)(2,1)S(1)}, u32[]{:S(2)}, u32[]{:S(2)}) collective-permute-start(bf16[384,384]{1,0:T(8,128)(2,1)S(1)} %constant_dynamic-update-slice_fusion.4.near), channel_id=1, source_target_pairs={{0,1},{1,0},{2,3},{3,2},{4,5},{5,4},{6,7},{7,6},{8,9},{9,8},{10,11... | collective-permute-start | bytes 884744 | tf_op jit(solution)/shard_map/ppermute | solution.py:289
  56.9 24.3 %collective-permute-start.8 = (bf16[384,384]{1,0:T(8,128)(2,1)S(1)}, bf16[384,384]{1,0:T(8,128)(2,1)S(1)}, u32[]{:S(2)}, u32[]{:S(2)}) collective-permute-start(bf16[384,384]{1,0:T(8,128)(2,1)S(1)} %constant_dynamic-update-slice_fusion.near), channel_id=1, source_target_pairs={{0,1},{1,0},{2,3},{3,2},{4,5},{5,4},{6,7},{7,6},{8,9},{9,8},{10,11... | collective-permute-start | bytes 884744 | tf_op jit(solution)/shard_map/ppermute | solution.py:289
  70.9 19.9 %collective-permute-start.19 = (bf16[512,128]{1,0:T(8,128)(2,1)}, bf16[512,128]{1,0:T(8,128)(2,1)S(1)}, u32[]{:S(2)}, u32[]{:S(2)}) collective-permute-start(bf16[512,128]{1,0:T(8,128)(2,1)} %get-tuple-element.63.o_other), channel_id=1, source_target_pairs={{0,16},{16,0},{1,17},{17,1},{2,18},{18,2},{3,19},{19,3},{4,20},{20... | collective-permute-start | bytes 393224 | tf_op jit(solution)/shard_map/ppermute | solution.py:400
  80.1 10.7 %collective-permute-start.18 = (bf16[512,128]{1,0:T(8,128)(2,1)}, bf16[512,128]{1,0:T(8,128)(2,1)S(1)}, u32[]{:S(2)}, u32[]{:S(2)}) collective-permute-start(bf16[512,128]{1,0:T(8,128)(2,1)} %get-tuple-element.62.o_other), channel_id=1, source_target_pairs={{0,16},{16,0},{1,17},{17,1},{2,18},{18,2},{3,19},{19,3},{4,20},{20... | collective-permute-start | bytes 393224 | tf_op jit(solution)/shard_map/ppermute | solution.py:400
  89.8 5.5 %collective-permute-start.17 = (bf16[512,128]{1,0:T(8,128)(2,1)}, bf16[512,128]{1,0:T(8,128)(2,1)S(1)}, u32[]{:S(2)}, u32[]{:S(2)}) collective-permute-start(bf16[512,128]{1,0:T(8,128)(2,1)} %get-tuple-element.61.o_other), channel_id=1, source_target_pairs={{0,16},{16,0},{1,17},{17,1},{2,18},{18,2},{3,19},{19,3},{4,20},{20... | collective-permute-start | bytes 393224 | tf_op jit(solution)/shard_map/ppermute | solution.py:400
  142.3 120.3 %collective-permute-start.49 = (bf16[384,3072]{1,0:T(8,128)(2,1)}, bf16[384,3072]{1,0:T(8,128)(2,1)}, u32[]{:S(2)}, u32[]{:S(2)}) collective-permute-start(bf16[384,3072]{1,0:T(8,128)(2,1)} %bitcast.148), channel_id=1, source_target_pairs={{0,1},{1,0},{2,3},{3,2},{4,5},{5,4},{6,7},{7,6},{8,9},{9,8},{10,11... | collective-permute-start | bytes 7077896 | tf_op jit(solution)/shard_map/ppermute | solution.py:289
  142.7 125.4 %collective-permute-start.43 = (bf16[384,3072]{1,0:T(8,128)(2,1)}, bf16[384,3072]{1,0:T(8,128)(2,1)S(1)}, u32[]{:S(2)}, u32[]{:S(2)}) collective-permute-start(bf16[384,3072]{1,0:T(8,128)(2,1)} %get-tuple-element.103), channel_id=1, source_target_pairs={{0,1},{1,0},{2,3},{3,2},{4,5},{5,4},{6,7},{7,6},{8,9},{9,8},{10,11... | collective-permute-start | bytes 7077896 | tf_op jit(solution)/shard_map/ppermute | solution.py:289
  148.2 6.9 %collective-permute-start.20 = (bf16[512,128]{1,0:T(8,128)(2,1)}, bf16[512,128]{1,0:T(8,128)(2,1)S(1)}, u32[]{:S(2)}, u32[]{:S(2)}) collective-permute-start(bf16[512,128]{1,0:T(8,128)(2,1)} %get-tuple-element.71), channel_id=1, source_target_pairs={{0,16},{16,0},{1,17},{17,1},{2,18},{18,2},{3,19},{19,3},{4,20},{20... | collective-permute-start | bytes 393224 | tf_op jit(solution)/shard_map/ppermute | solution.py:469
  152.9 88.7 %collective-permute-start.37 = (bf16[384,768]{1,0:T(8,128)(2,1)}, bf16[384,768]{1,0:T(8,128)(2,1)S(1)}, u32[]{:S(2)}, u32[]{:S(2)}) collective-permute-start(bf16[384,768]{1,0:T(8,128)(2,1)} %get-tuple-element.101), channel_id=1, source_target_pairs={{0,1},{1,0},{2,3},{3,2},{4,5},{5,4},{6,7},{7,6},{8,9},{9,8},{10,11... | collective-permute-start | bytes 1769480 | tf_op jit(solution)/shard_map/ppermute | solution.py:289
  154.5 11.1 %collective-permute-start.21 = (bf16[512,128]{1,0:T(8,128)(2,1)S(1)}, bf16[512,128]{1,0:T(8,128)(2,1)S(1)}, u32[]{:S(2)}, u32[]{:S(2)}) collective-permute-start(bf16[512,128]{1,0:T(8,128)(2,1)S(1)} %copy-done.33), channel_id=1, source_target_pairs={{0,16},{16,0},{1,17},{17,1},{2,18},{18,2},{3,19},{19,3},{4,20},{20... | collective-permute-start | bytes 393224 | tf_op jit(solution)/shard_map/ppermute | solution.py:469
  155.1 20.5 %collective-permute-start.22 = (bf16[512,128]{1,0:T(8,128)(2,1)S(1)}, bf16[512,128]{1,0:T(8,128)(2,1)S(1)}, u32[]{:S(2)}, u32[]{:S(2)}) collective-permute-start(bf16[512,128]{1,0:T(8,128)(2,1)S(1)} %copy-done.30), channel_id=1, source_target_pairs={{0,16},{16,0},{1,17},{17,1},{2,18},{18,2},{3,19},{19,3},{4,20},{20... | collective-permute-start | bytes 393224 | tf_op jit(solution)/shard_map/ppermute | solution.py:469
  165.7 28.1 %collective-permute-start.24 = (bf16[384,384]{1,0:T(8,128)(2,1)}, bf16[384,384]{1,0:T(8,128)(2,1)S(1)}, u32[]{:S(2)}, u32[]{:S(2)}) collective-permute-start(bf16[384,384]{1,0:T(8,128)(2,1)} %get-tuple-element.93), channel_id=1, source_target_pairs={{0,1},{1,0},{2,3},{3,2},{4,5},{5,4},{6,7},{7,6},{8,9},{9,8},{10,11... | collective-permute-start | bytes 884744 | tf_op jit(solution)/shard_map/ppermute | solution.py:289
  175.6 18.3 %collective-permute-start.28 = (bf16[384,384]{1,0:T(8,128)(2,1)}, bf16[384,384]{1,0:T(8,128)(2,1)S(1)}, u32[]{:S(2)}, u32[]{:S(2)}) collective-permute-start(bf16[384,384]{1,0:T(8,128)(2,1)} %get-tuple-element.95), channel_id=1, source_target_pairs={{0,1},{1,0},{2,3},{3,2},{4,5},{5,4},{6,7},{7,6},{8,9},{9,8},{10,11... | collective-permute-start | bytes 884744 | tf_op jit(solution)/shard_map/ppermute | solution.py:289
  193.9 92.1 %collective-permute-start.23 = (bf16[512,768]{1,0:T(8,128)(2,1)}, bf16[512,768]{1,0:T(8,128)(2,1)}, u32[]{:S(2)}, u32[]{:S(2)}) collective-permute-start(bf16[512,768]{1,0:T(8,128)(2,1)} %token_back.1), channel_id=1, source_target_pairs={{0,16},{16,0},{1,17},{17,1},{2,18},{18,2},{3,19},{19,3},{4,20},{20... | collective-permute-start | bytes 2359304 | tf_op jit(solution)/shard_map/ppermute | solution.py:507
  195.4 5.9 %collective-permute-start.25 = (bf16[2,2,1,48,384]{4,3,2,1,0:T(8,128)(2,1)S(1)}, bf16[2,2,1,48,384]{4,3,2,1,0:T(8,128)(2,1)S(1)}, u32[]{:S(2)}, u32[]{:S(2)}) collective-permute-start(bf16[2,2,1,48,384]{4,3,2,1,0:T(8,128)(2,1)S(1)} %add_convert_fusion.14), channel_id=1, source_target_pairs={{0,2},{1,3},{2,0},{3,1},{4,6},{5,7},{6,4},{7,5},{8,10},{9,11},{10,... | collective-permute-start | bytes 442376 | tf_op jit(solution)/shard_map/ppermute | solution.py:289
  201.3 5.2 %collective-permute-start.29 = (bf16[2,2,1,48,384]{4,3,2,1,0:T(8,128)(2,1)S(1)}, bf16[2,2,1,48,384]{4,3,2,1,0:T(8,128)(2,1)S(1)}, u32[]{:S(2)}, u32[]{:S(2)}) collective-permute-start(bf16[2,2,1,48,384]{4,3,2,1,0:T(8,128)(2,1)S(1)} %add_convert_fusion.13), channel_id=1, source_target_pairs={{0,2},{1,3},{2,0},{3,1},{4,6},{5,7},{6,4},{7,5},{8,10},{9,11},{10,... | collective-permute-start | bytes 442376 | tf_op jit(solution)/shard_map/ppermute | solution.py:289
  206.5 5.1 %collective-permute-start.33 = (bf16[2,2,1,48,384]{4,3,2,1,0:T(8,128)(2,1)S(1)}, bf16[2,2,1,48,384]{4,3,2,1,0:T(8,128)(2,1)S(1)}, u32[]{:S(2)}, u32[]{:S(2)}) collective-permute-start(bf16[2,2,1,48,384]{4,3,2,1,0:T(8,128)(2,1)S(1)} %add_convert_fusion.12), channel_id=1, source_target_pairs={{0,2},{1,3},{2,0},{3,1},{4,6},{5,7},{6,4},{7,5},{8,10},{9,11},{10,... | collective-permute-start | bytes 442376 | tf_op jit(solution)/shard_map/ppermute | solution.py:289
  225.2 5.1 %collective-permute-start.27 = (bf16[1,1,1,48,384]{4,3,2,1,0:T(8,128)(2,1)S(1)}, bf16[1,1,1,48,384]{4,3,2,1,0:T(8,128)(2,1)S(1)}, u32[]{:S(2)}, u32[]{:S(2)}) collective-permute-start(bf16[1,1,1,48,384]{4,3,2,1,0:T(8,128)(2,1)S(1)} %add_convert_fusion.26), channel_id=1, source_target_pairs={{0,8},{1,9},{2,10},{3,11},{4,12},{5,13},{6,14},{7,15},{8,0},{9,1},... | collective-permute-start | bytes 110600 | tf_op jit(solution)/shard_map/ppermute | solution.py:289
  230.3 4.9 %collective-permute-start.31 = (bf16[1,1,1,48,384]{4,3,2,1,0:T(8,128)(2,1)S(1)}, bf16[1,1,1,48,384]{4,3,2,1,0:T(8,128)(2,1)S(1)}, u32[]{:S(2)}, u32[]{:S(2)}) collective-permute-start(bf16[1,1,1,48,384]{4,3,2,1,0:T(8,128)(2,1)S(1)} %add_convert_fusion.24), channel_id=1, source_target_pairs={{0,8},{1,9},{2,10},{3,11},{4,12},{5,13},{6,14},{7,15},{8,0},{9,1},... | collective-permute-start | bytes 110600 | tf_op jit(solution)/shard_map/ppermute | solution.py:289
  235.2 5.2 %collective-permute-start.35 = (bf16[1,1,1,48,384]{4,3,2,1,0:T(8,128)(2,1)S(1)}, bf16[1,1,1,48,384]{4,3,2,1,0:T(8,128)(2,1)S(1)}, u32[]{:S(2)}, u32[]{:S(2)}) collective-permute-start(bf16[1,1,1,48,384]{4,3,2,1,0:T(8,128)(2,1)S(1)} %add_convert_fusion.22), channel_id=1, source_target_pairs={{0,8},{1,9},{2,10},{3,11},{4,12},{5,13},{6,14},{7,15},{8,0},{9,1},... | collective-permute-start | bytes 110600 | tf_op jit(solution)/shard_map/ppermute | solution.py:289
  243.1 10.7 %collective-permute-start.38 = (bf16[2,1,2,48,768]{4,3,2,1,0:T(8,128)(2,1)}, bf16[2,1,2,48,768]{4,3,2,1,0:T(8,128)(2,1)}, u32[]{:S(2)}, u32[]{:S(2)}) collective-permute-start(bf16[2,1,2,48,768]{4,3,2,1,0:T(8,128)(2,1)} %add_convert_fusion.6), channel_id=1, source_target_pairs={{0,4},{1,5},{2,6},{3,7},{4,0},{5,1},{6,2},{7,3},{8,12},{9,13},{10,... | collective-permute-start | bytes 884744 | tf_op jit(solution)/shard_map/ppermute | solution.py:289
  255.0 6.8 %collective-permute-start.39 = (bf16[2,1,1,48,768]{4,3,2,1,0:T(8,128)(2,1)S(1)}, bf16[2,1,1,48,768]{4,3,2,1,0:T(8,128)(2,1)S(1)}, u32[]{:S(2)}, u32[]{:S(2)}) collective-permute-start(bf16[2,1,1,48,768]{4,3,2,1,0:T(8,128)(2,1)S(1)} %add_convert_fusion.11), channel_id=1, source_target_pairs={{0,2},{1,3},{2,0},{3,1},{4,6},{5,7},{6,4},{7,5},{8,10},{9,11},{10,... | collective-permute-start | bytes 442376 | tf_op jit(solution)/shard_map/ppermute | solution.py:289
  261.8 5.3 %collective-permute-start.40 = (bf16[2,1,1,48,384]{4,3,2,1,0:T(8,128)(2,1)S(1)}, bf16[2,1,1,48,384]{4,3,2,1,0:T(8,128)(2,1)S(1)}, u32[]{:S(2)}, u32[]{:S(2)}) collective-permute-start(bf16[2,1,1,48,384]{4,3,2,1,0:T(8,128)(2,1)S(1)} %add_convert_fusion.15), channel_id=1, source_target_pairs={{0,16},{16,0},{1,17},{17,1},{2,18},{18,2},{3,19},{19,3},{4,20},{20... | collective-permute-start | bytes 221192 | tf_op jit(solution)/shard_map/ppermute | solution.py:308
  264.7 18.0 %collective-permute-start.50 = (bf16[2,2,2,48,1536]{4,3,2,1,0:T(8,128)(2,1)S(1)}, bf16[2,2,2,48,1536]{4,3,2,1,0:T(8,128)(2,1)S(1)}, u32[]{:S(2)}, u32[]{:S(2)}) collective-permute-start(bf16[2,2,2,48,1536]{4,3,2,1,0:T(8,128)(2,1)S(1)} %add_convert_fusion), channel_id=1, source_target_pairs={{0,16},{16,0},{1,17},{17,1},{2,18},{18,2},{3,19},{19,3},{4,20},{20... | collective-permute-start | bytes 3538952 | tf_op jit(solution)/shard_map/ppermute | solution.py:308
  267.1 4.9 %collective-permute-start.41 = (bf16[1,1,1,48,384]{4,3,2,1,0:T(8,128)(2,1)S(1)}, bf16[1,1,1,48,384]{4,3,2,1,0:T(8,128)(2,1)S(1)}, u32[]{:S(2)}, u32[]{:S(2)}) collective-permute-start(bf16[1,1,1,48,384]{4,3,2,1,0:T(8,128)(2,1)S(1)} %add_convert_fusion.20), channel_id=1, source_target_pairs={{0,8},{1,9},{2,10},{3,11},{4,12},{5,13},{6,14},{7,15},{8,0},{9,1},... | collective-permute-start | bytes 110600 | tf_op jit(solution)/shard_map/ppermute | solution.py:289
  269.5 21.2 %collective-permute-start.44 = (bf16[2,2,1,48,3072]{4,3,2,1,0:T(8,128)(2,1)}, bf16[2,2,1,48,3072]{4,3,2,1,0:T(8,128)(2,1)S(1)}, u32[]{:S(2)}, u32[]{:S(2)}) collective-permute-start(bf16[2,2,1,48,3072]{4,3,2,1,0:T(8,128)(2,1)} %add_convert_fusion.1), channel_id=1, source_target_pairs={{0,2},{1,3},{2,0},{3,1},{4,6},{5,7},{6,4},{7,5},{8,10},{9,11},{10,... | collective-permute-start | bytes 3538952 | tf_op jit(solution)/shard_map/ppermute | solution.py:289
  272.1 18.5 %collective-permute-start.42 = (bf16[48,384]{1,0:T(8,128)(2,1)S(1)}, bf16[48,384]{1,0:T(8,128)(2,1)S(1)}, u32[]{:S(2)}, u32[]{:S(2)}) collective-permute-start(bf16[48,384]{1,0:T(8,128)(2,1)S(1)} %bitcast.140), channel_id=1, source_target_pairs={{0,16},{16,0},{1,17},{17,1},{2,18},{18,2},{3,19},{19,3},{4,20},{20... | collective-permute-start | bytes 110600 | tf_op jit(solution)/shard_map/ppermute | solution.py:319
  285.9 14.9 %collective-permute-start.51 = (bf16[2,1,2,48,1536]{4,3,2,1,0:T(8,128)(2,1)}, bf16[2,1,2,48,1536]{4,3,2,1,0:T(8,128)(2,1)}, u32[]{:S(2)}, u32[]{:S(2)}) collective-permute-start(bf16[2,1,2,48,1536]{4,3,2,1,0:T(8,128)(2,1)} %add_convert_fusion.2), channel_id=1, source_target_pairs={{0,4},{1,5},{2,6},{3,7},{4,0},{5,1},{6,2},{7,3},{8,12},{9,13},{10,... | collective-permute-start | bytes 1769480 | tf_op jit(solution)/shard_map/ppermute | solution.py:289
  291.0 11.5 %collective-permute-start.45 = (bf16[2,2,1,48,1536]{4,3,2,1,0:T(8,128)(2,1)S(1)}, bf16[2,2,1,48,1536]{4,3,2,1,0:T(8,128)(2,1)S(1)}, u32[]{:S(2)}, u32[]{:S(2)}) collective-permute-start(bf16[2,2,1,48,1536]{4,3,2,1,0:T(8,128)(2,1)S(1)} %add_convert_fusion.3), channel_id=1, source_target_pairs={{0,16},{16,0},{1,17},{17,1},{2,18},{18,2},{3,19},{19,3},{4,20},{20... | collective-permute-start | bytes 1769480 | tf_op jit(solution)/shard_map/ppermute | solution.py:308
  302.0 6.8 %collective-permute-start.52 = (bf16[2,1,1,48,1536]{4,3,2,1,0:T(8,128)(2,1)S(1)}, bf16[2,1,1,48,1536]{4,3,2,1,0:T(8,128)(2,1)S(1)}, u32[]{:S(2)}, u32[]{:S(2)}) collective-permute-start(bf16[2,1,1,48,1536]{4,3,2,1,0:T(8,128)(2,1)S(1)} %add_convert_fusion.4), channel_id=1, source_target_pairs={{0,2},{1,3},{2,0},{3,1},{4,6},{5,7},{6,4},{7,5},{8,10},{9,11},{10,... | collective-permute-start | bytes 884744 | tf_op jit(solution)/shard_map/ppermute | solution.py:289
  302.8 7.2 %collective-permute-start.46 = (bf16[2,1,1,48,1536]{4,3,2,1,0:T(8,128)(2,1)S(1)}, bf16[2,1,1,48,1536]{4,3,2,1,0:T(8,128)(2,1)S(1)}, u32[]{:S(2)}, u32[]{:S(2)}) collective-permute-start(bf16[2,1,1,48,1536]{4,3,2,1,0:T(8,128)(2,1)S(1)} %add_convert_fusion.5), channel_id=1, source_target_pairs={{0,4},{1,5},{2,6},{3,7},{4,0},{5,1},{6,2},{7,3},{8,12},{9,13},{10,... | collective-permute-start | bytes 884744 | tf_op jit(solution)/shard_map/ppermute | solution.py:289
  309.9 8.7 %collective-permute-start.53 = (bf16[1,1,1,48,1536]{4,3,2,1,0:T(8,128)(2,1)S(1)}, bf16[1,1,1,48,1536]{4,3,2,1,0:T(8,128)(2,1)S(1)}, u32[]{:S(2)}, u32[]{:S(2)}) collective-permute-start(bf16[1,1,1,48,1536]{4,3,2,1,0:T(8,128)(2,1)S(1)} %add_convert_fusion.8), channel_id=1, source_target_pairs={{0,8},{1,9},{2,10},{3,11},{4,12},{5,13},{6,14},{7,15},{8,0},{9,1},... | collective-permute-start | bytes 442376 | tf_op jit(solution)/shard_map/ppermute | solution.py:289
  310.1 11.5 %collective-permute-start.47 = (bf16[1,1,1,48,1536]{4,3,2,1,0:T(8,128)(2,1)S(1)}, bf16[1,1,1,48,1536]{4,3,2,1,0:T(8,128)(2,1)S(1)}, u32[]{:S(2)}, u32[]{:S(2)}) collective-permute-start(bf16[1,1,1,48,1536]{4,3,2,1,0:T(8,128)(2,1)S(1)} %add_convert_fusion.10), channel_id=1, source_target_pairs={{0,8},{1,9},{2,10},{3,11},{4,12},{5,13},{6,14},{7,15},{8,0},{9,1},... | collective-permute-start | bytes 442376 | tf_op jit(solution)/shard_map/ppermute | solution.py:289
  319.7 5.2 %collective-permute-start.54 = (bf16[48,1536]{1,0:T(8,128)(2,1)S(1)}, bf16[48,1536]{1,0:T(8,128)(2,1)S(1)}, u32[]{:S(2)}, u32[]{:S(2)}) collective-permute-start(bf16[48,1536]{1,0:T(8,128)(2,1)S(1)} %bitcast.98), channel_id=1, source_target_pairs={{0,16},{16,0},{1,17},{17,1},{2,18},{18,2},{3,19},{19,3},{4,20},{20... | collective-permute-start | bytes 442376 | tf_op jit(solution)/shard_map/ppermute | solution.py:319
  321.7 5.3 %collective-permute-start.48 = (bf16[48,1536]{1,0:T(8,128)(2,1)S(1)}, bf16[48,1536]{1,0:T(8,128)(2,1)S(1)}, u32[]{:S(2)}, u32[]{:S(2)}) collective-permute-start(bf16[48,1536]{1,0:T(8,128)(2,1)S(1)} %bitcast.100), channel_id=1, source_target_pairs={{0,16},{16,0},{1,17},{17,1},{2,18},{18,2},{3,19},{19,3},{4,20},{20... | collective-permute-start | bytes 442376 | tf_op jit(solution)/shard_map/ppermute | solution.py:319
  (44 other events, 207.9 us)
Sparse Core Ops, SparseCore 0:
  11.9 96.2 all-gather.1
